TPU v7x, 32 devices: a whole 2x2x4 slice. The times are simulated.
32 devices in a mesh: group: 4 (over z), dev: 8 (over y, x, core).
Axes of the slice: x: 2, y: 2, z: 4, core: 2. Of those that a mesh axis runs over, the one named last changes fastest.
Arguments:
- fine_state: float32 [5, 128, 16384], P(None, 'group', 'dev'), may hold values from -2 to 9.25, as said below
- coarse_boxes: float32 [4096, 5, 512], P(('group', 'dev')), may hold values from -2 to 9.25, as said below
- piece_owner: int32 [1024, 1], P(('group', 'dev')), may hold values from 0 to 7; in each aligned block of 32 rows (0 to 31, 32 to 63, ...) at most 8 rows name the same one
- piece_box: int32 [1024], P(('group', 'dev')), may hold values from 0 to 127
Outputs:
- fine_next: float32 [5, 128, 16384], P(None, 'group', 'dev')
- flux_register: float32 [5, 32, 4096], P(None, None, ('group', 'dev'))
Inputs may be any that keep to these rules, and one draw needn't show every extreme that they name: `piece_owner`: among the pieces of one device no owner is named more than 8 times, and in some devices one owner is named exactly 8 times. `fine_state`: conserved variables of states with density in 0.5 to 2, velocity components in -1 to 1 and pressure in 0.4 to 2.5. `coarse_boxes`: conserved variables of states with density in 0.5 to 2, velocity components in -1 to 1 and pressure in 0.4 to 2.5.
All inputs are finite; a program needn't handle non-finite values.
Results may differ from a plain program's by a relative error of at most 0.0003.
Values sent between devices are 32-bit elements; how exact they have to be, the bound alone decides.
No kernel may reach another device: no remote copies, remote signals or barrier semaphores. Data moves between devices by JAX's collectives and lax.ppermute only.
A program may use at most 128 MiB of HBM per device.

v0:
```python
import jax
import jax.numpy as jnp
from jax import lax
from jax.sharding import PartitionSpec as P

PS = 16
RATIO = 4
QS = 16
PATCH_Y = 2
PATCH_X = 8
BOX_DEV = 128
CF = 4
CB = 8


GAMMA = 1.4
DT_DX = 0.08


def with_halo(block, sides, width, periodic):
    for axis, dim in sides:
        count = lax.axis_size(axis)
        forward = [(i, i + 1) for i in range(count - 1)]
        if periodic:
            forward.append((count - 1, 0))
        backward = [(target, source) for source, target in forward]
        low = lax.ppermute(
            lax.slice_in_dim(block, block.shape[dim] - width, None, axis=dim), axis, forward
        )
        high = lax.ppermute(lax.slice_in_dim(block, 0, width, axis=dim), axis, backward)
        block = jnp.concatenate([low, block, high], axis=dim)
    return block


def minmod(lower_diff, upper_diff):
    return jnp.where(
        lower_diff * upper_diff > 0.0,
        jnp.where(jnp.abs(lower_diff) < jnp.abs(upper_diff), lower_diff, upper_diff),
        0.0,
    )


def to_primitive(conserved):
    density = conserved[0]
    momentum = conserved[1:4]
    kinetic = (
        0.5
        * (momentum[0] * momentum[0] + momentum[1] * momentum[1] + momentum[2] * momentum[2])
        / density
    )
    pressure = (GAMMA - 1.0) * (conserved[4] - kinetic)
    return jnp.stack(
        [density, momentum[0] / density, momentum[1] / density, momentum[2] / density, pressure]
    )


def state_terms(primitive, normal):
    density = primitive[0]
    pressure = primitive[4]
    normal_speed = primitive[1 + normal]
    energy = pressure / (GAMMA - 1.0) + 0.5 * density * (
        primitive[1] * primitive[1] + primitive[2] * primitive[2] + primitive[3] * primitive[3]
    )
    cons_list = [
        density,
        density * primitive[1],
        density * primitive[2],
        density * primitive[3],
        energy,
    ]
    flux_list = [element * normal_speed for element in cons_list]
    flux_list[1 + normal] = flux_list[1 + normal] + pressure
    flux_list[4] = flux_list[4] + pressure * normal_speed
    sound_speed = jnp.sqrt(GAMMA * pressure / density)
    return (jnp.stack(cons_list), jnp.stack(flux_list), normal_speed, sound_speed)


def hll_flux(lower_state, upper_state, normal):
    cons_low, flux_low, speed_low, sound_low = state_terms(lower_state, normal)
    cons_up, flux_up, speed_up, sound_up = state_terms(upper_state, normal)
    slowest = jnp.minimum(jnp.minimum(speed_low - sound_low, speed_up - sound_up), 0.0)
    fastest = jnp.maximum(jnp.maximum(speed_low + sound_low, speed_up + sound_up), 0.0)
    return (fastest * flux_low - slowest * flux_up + slowest * fastest * (cons_up - cons_low)) / (
        fastest - slowest
    )


def face_fluxes(primitive, lower_ghost, upper_ghost, dim_index, normal):
    length = primitive.shape[dim_index]

    def part_of(array, start, stop):
        return lax.slice_in_dim(array, start, stop, axis=dim_index)

    before = jnp.concatenate(
        [part_of(lower_ghost, 1, 2), part_of(primitive, 0, length - 1)], axis=dim_index
    )
    before_two = jnp.concatenate([lower_ghost, part_of(primitive, 0, length - 2)], axis=dim_index)
    after = jnp.concatenate(
        [part_of(primitive, 1, length), part_of(upper_ghost, 0, 1)], axis=dim_index
    )
    slopes = minmod(primitive - before, after - primitive)
    slopes_before = minmod(before - before_two, primitive - before)
    lower_faces = hll_flux(before + 0.5 * slopes_before, primitive - 0.5 * slopes, normal)
    last_cell = part_of(primitive, length - 1, length)
    ghost_near = part_of(upper_ghost, 0, 1)
    ghost_far = part_of(upper_ghost, 1, 2)
    ghost_slope = minmod(ghost_near - last_cell, ghost_far - ghost_near)
    end_face = hll_flux(
        last_cell + 0.5 * part_of(slopes, length - 1, length),
        ghost_near - 0.5 * ghost_slope,
        normal,
    )
    upper_faces = jnp.concatenate([part_of(lower_faces, 1, length), end_face], axis=dim_index)
    return (upper_faces - lower_faces, lower_faces, end_face)


def advance(primitive, x_low, x_high, y_low, y_high, z_low, z_high):
    change = (
        face_fluxes(primitive, x_low, x_high, 3, 0)[0]
        + face_fluxes(primitive, y_low, y_high, 1, 1)[0]
    )
    z_change, z_lower, z_end = face_fluxes(primitive, z_low, z_high, 2, 2)
    return (change + z_change, z_lower[:, :, 0, :], z_end[:, :, 0, :])


def extract(box_cells, face_side):
    shaped = box_cells.reshape(box_cells.shape[:-1] + (CB, CB, CB))
    low_cut = shaped[..., CB - 4 : CB - 1, 1 : CB - 1, 1 : CB - 1]
    high_cut = shaped[..., 1:4, 1 : CB - 1, 1 : CB - 1]
    return jnp.where((face_side == 1)[..., None, None, None, None], high_cut, low_cut)


def spread(values):
    return values[..., None, :, None, :, None]


def interpolate(coarse_cut, face_side):
    moved = jnp.moveaxis(coarse_cut, -4, 0)
    primitive = to_primitive(moved)
    centre = primitive[..., 1, 1:-1, 1:-1]
    slope_z = minmod(centre - primitive[..., 0, 1:-1, 1:-1], primitive[..., 2, 1:-1, 1:-1] - centre)
    slope_y = minmod(centre - primitive[..., 1, :-2, 1:-1], primitive[..., 1, 2:, 1:-1] - centre)
    slope_x = minmod(centre - primitive[..., 1, 1:-1, :-2], primitive[..., 1, 1:-1, 2:] - centre)
    offsets = (jnp.arange(RATIO, dtype=jnp.float32) + 0.5) / RATIO - 0.5
    z_offsets = jnp.where((face_side == 1)[..., None], offsets[:2], offsets[RATIO - 2 :])
    fine = spread(centre) + spread(slope_z) * z_offsets[..., :, None, None, None, None]
    fine = fine + spread(slope_y) * offsets[:, None, None]
    fine = fine + spread(slope_x) * offsets
    fine = fine.reshape(fine.shape[:-5] + (2, QS, QS))
    return jnp.moveaxis(fine, 0, -4)


def assemble(pieces, face_index):
    chosen = pieces[:, :, face_index]
    return chosen.transpose(4, 0, 3, 6, 5, 1, 2, 7).reshape(5, PATCH_Y * PS, 2, PATCH_X * PS)


def coarsen(flux):
    across = PS // QS
    grouped = flux.reshape(5, PATCH_Y, across, CF, RATIO, PATCH_X, across, CF, RATIO)
    summed = grouped.sum(axis=(4, 8)) * (1.0 / RATIO)
    return summed.transpose(1, 4, 5, 2, 0, 3, 6)


def local(fine_state, coarse_boxes, piece_owner, piece_box):
    members = lax.axis_size("dev")
    dev_index = lax.axis_index("dev")
    y_cells = fine_state.shape[1]
    x_cells = fine_state.shape[2] // PS
    across = PS // QS
    conserved = fine_state.reshape(5, y_cells, x_cells, PS).transpose(0, 1, 3, 2)
    primitive = to_primitive(conserved)
    x_edges = jnp.concatenate([primitive[..., :2], primitive[..., x_cells - 2 :]], axis=3)
    x_wide = with_halo(x_edges, (("dev", 3),), 2, False)
    first_cell = primitive[..., :1]
    last_cell = primitive[..., x_cells - 1 :]
    x_low = jnp.where(
        dev_index == 0, jnp.concatenate([first_cell, first_cell], axis=3), x_wide[..., :2]
    )
    x_high = jnp.where(
        dev_index == members - 1, jnp.concatenate([last_cell, last_cell], axis=3), x_wide[..., 6:]
    )
    y_edges = jnp.concatenate([primitive[:, :2], primitive[:, y_cells - 2 :]], axis=1)
    y_wide = with_halo(y_edges, (("group", 1),), 2, True)
    y_low = y_wide[:, :2]
    y_high = y_wide[:, 6:]
    piece_count = piece_box.shape[0]
    capacity = max(4, 2 * piece_count // members)
    owners = piece_owner[:, 0]
    local_ids = jnp.arange(piece_count, dtype=jnp.int32)
    face_side = local_ids // (across * across) % 2
    request_value = piece_box + BOX_DEV * face_side
    owner_hot = (owners[:, None] == jnp.arange(members, dtype=jnp.int32)[None, :]).astype(jnp.int32)
    earlier = jnp.cumsum(owner_hot, axis=0) - owner_hot
    ranks = jnp.sum(earlier * owner_hot, axis=1)
    slot_ids = owners * capacity + ranks
    slot_hot = slot_ids[:, None] == jnp.arange(members * capacity, dtype=jnp.int32)[None, :]
    requests = (jnp.sum(jnp.where(slot_hot, request_value[:, None] + 1, 0), axis=0) - 1).reshape(
        members, capacity
    )
    received = lax.all_to_all(requests, "dev", split_axis=0, concat_axis=0, tiled=True)
    slot_live = received >= 0
    box_local = jnp.where(slot_live, received % BOX_DEV, 0)
    served_side = jnp.where(slot_live, received // BOX_DEV, 0)
    coarse_cut = extract(coarse_boxes[box_local], served_side)
    payload = jnp.where(slot_live[..., None, None, None, None], coarse_cut, 0.0)
    back = lax.all_to_all(payload, "dev", split_axis=0, concat_axis=0, tiled=True)
    flat = back.reshape((members * capacity,) + back.shape[2:])
    mine = flat[slot_ids]
    ghost_cells = interpolate(mine, face_side)
    pieces = ghost_cells.reshape(PATCH_Y, PATCH_X, 2, across, across, 5, 2, QS, QS)
    z_low = assemble(pieces, 0)
    z_high = assemble(pieces, 1)
    change, bottom_flux, top_flux = advance(primitive, x_low, x_high, y_low, y_high, z_low, z_high)
    fine_next = (conserved - DT_DX * change).transpose(0, 1, 3, 2).reshape(5, y_cells, x_cells * PS)
    register_terms = jnp.stack([coarsen(bottom_flux), coarsen(top_flux)], axis=2).reshape(
        piece_count, 5 * CF * CF
    )
    outgoing = jnp.dot(
        slot_hot.astype(jnp.float32).T,
        register_terms,
        precision=lax.Precision.HIGHEST,
        preferred_element_type=jnp.float32,
    )
    incoming = lax.all_to_all(
        outgoing.reshape(members, capacity, 5 * CF * CF),
        "dev",
        split_axis=0,
        concat_axis=0,
        tiled=True,
    )
    targets = received.reshape(members * capacity)
    target_hot = (targets[:, None] == jnp.arange(2 * BOX_DEV, dtype=jnp.int32)[None, :]).astype(
        jnp.float32
    )
    summed = jnp.dot(
        incoming.reshape(members * capacity, 5 * CF * CF).T,
        target_hot,
        precision=lax.Precision.HIGHEST,
        preferred_element_type=jnp.float32,
    )
    flux_register = (
        summed.reshape(5, CF * CF, 2, BOX_DEV)
        .transpose(0, 2, 1, 3)
        .reshape(5, 2 * CF * CF, BOX_DEV)
    )
    return (fine_next, flux_register)


def solution(mesh):
    in_specs = (
        P(None, "group", "dev"),
        P(("group", "dev"), None, None),
        P(("group", "dev"), None),
        P(("group", "dev")),
    )
    out_specs = (P(None, "group", "dev"), P(None, None, ("group", "dev")))
    return jax.shard_map(local, mesh=mesh, in_specs=in_specs, out_specs=out_specs, check_vma=False)
```

profile of v0, /device:TPU:0, one launch (start us, length us, event | category | flops | bytes accessed | tf_op | source)
XLA Modules:
  0.0 305.8 jit_solution(14255506862372514953)
XLA Ops:
  4.5 5.2 %all-to-all-start = ((s32[8,1,8]{2,1,0:T(1,128)}), s32[8,1,8]{2,1,0:T(1,128)S(1)}, u32[]{:S(2)}, u32[]{:S(2)}) async-start(s32[8,1,8]{2,1,0:T(1,128)} %bitcast.25), calls=%async_computation | async-start | bytes 8192 | tf_op jit(solution)/shard_map/all_to_all | solution.py:201
  9.7 4.5 %copy.1218 = f32[5,32,2048]{1,2,0:T(8,128)} copy(f32[5,32,2048]{2,1,0:T(8,128)} %param.4) | data formatting | bytes 2621440 | tf_op args[0]
  14.2 5.4 %copy.1219 = f32[5,32,128,16]{2,3,1,0:T(8,128)} copy(f32[5,32,128,16]{1,3,2,0:T(8,128)} %bitcast.210) | data formatting | bytes 2621440 | tf_op jit(solution)/shard_map/reshape | solution.py:171
  24.2 2.2 collective-permute-start.3
  28.4 2.5 copy.1220
  30.9 2.5 collective-permute-start
  49.3 7.4 %reshape.2071 = f32[8,8,5,8,8,8]{5,4,3,1,0,2:T(8,128)} reshape(f32[64,5,512]{2,0,1:T(8,128)S(1)} %gather_fusion) | data formatting | bytes 1310720 | tf_op jit(solution)/shard_map/reshape | solution.py:127
  56.8 5.4 %fusion.56 = (f32[8,8,5,3,6,6]{5,4,3,1,0,2:T(8,128)S(1)}, f32[8,8,5,3,6,6]{5,4,3,1,0,2:T(8,128)S(1)}) fusion(f32[8,8,5,8,8,8]{5,4,3,1,0,2:T(8,128)} %reshape.2071), kind=kLoop, calls=%fused_computation.409 | loop fusion | bytes 552960 | tf_op jit(solution)/shard_map/slice | solution.py:129
  62.2 3.1 %fusion.72 = f32[8,5,3,6,8,6]{5,4,3,2,1,0:T(8,128)} fusion(f32[8,8,5,3,6,6]{5,4,3,1,0,2:T(8,128)S(1)} %get-tuple-element.112, f32[8,8,5,3,6,6]{5,4,3,1,0,2:T(8,128)S(1)} %get-tuple-element.111, pred[8,8]{1,0:T(8,128)(4,1)S(1)} %get-tuple-element.237, pred[8,8]{1,0:T(8,128)(4,1)S(1)} %get-tuple-element.236), kind=kLoop, calls=%fused_computation.425 | loop fusion | flops 69120 | bytes 414848
  65.3 4.3 %reshape.2270 = f32[8,1,4320]{2,1,0:T(1,128)} reshape(f32[8,5,3,6,8,6]{5,4,3,2,1,0:T(8,128)} %fusion.72) | data formatting | bytes 276480
  69.6 6.1 %all-to-all-start.1 = ((f32[8,1,4320]{2,1,0:T(1,128)}), f32[8,1,4320]{2,1,0:T(1,128)S(1)}, u32[]{:S(2)}, u32[]{:S(2)}) async-start(f32[8,1,4320]{2,1,0:T(1,128)} %reshape.2270), calls=%async_computation.1 | async-start | bytes 278528 | tf_op jit(solution)/shard_map/all_to_all | solution.py:207
  77.6 2.5 copy.1221
  80.1 2.3 maximum_select_fusion
  83.8 2.6 copy.1223
  89.0 3.8 %multiply_subtract_fusion.3 = (f32[5,32,16,128]{3,2,1,0:T(8,128)S(1)}, f32[5,32,16,128]{3,2,1,0:T(8,128)S(1)}, f32[5,32,16,128]{3,2,1,0:T(8,128)}) fusion(f32[5,32,16,128]{3,2,1,0:T(8,128)S(1)} %constant_dynamic-update-slice_fusion, f32[5,32,16,1]{3,2,1,0:T(8,128)S(1)} %bitcast.211, f32[5,32,16,127]{3,2,1,0:T(8,128)S(1)} %copy-done.15, ...), kind=kLoop, calls=%fused_computation.51 | loop fusion | flops 7536640 | bytes 9175040 | tf_op jit(solution)/shard_map/sub | solution.py:103
  99.8 3.4 %fusion.55 = (f32[1,32,16,1]{3,2,1,0:T(8,128)S(1)}, f32[1,32,16,1]{3,2,1,0:T(8,128)S(1)}, f32[1,32,16,1]{3,2,1,0:T(8,128)S(1)}, f32[5,32,16,1]{3,2,1,0:T(8,128)}...) fusion(f32[1,32,16,1]{3,2,1,0:T(8,128)} %copy.1229, ...), kind=kLoop, calls=%fused_computation.408 | loop fusion | flops 6654 | bytes 3172352 | tf_op jit(solution)/shard_map/mul | solution.py:83
  124.7 2.2 constant_dynamic-update-slice_fusion.36
  153.3 3.0 sub.398
  168.0 3.1 %reshape.2271 = f32[8,5,3,6,8,6]{5,4,3,2,1,0:T(8,128)} reshape(f32[8,4320]{1,0:T(8,128)S(1)} %reduce.118) | data formatting | bytes 276480
  171.1 4.5 %copy.1329 = f32[8,8,5,3,6,6]{5,4,3,2,1,0:T(8,128)} copy(f32[8,8,5,3,6,6]{5,1,4,3,2,0:T(8,128)} %bitcast.212) | data formatting | bytes 276480 | tf_op jit(solution)/shard_map/reshape | solution.py:208
  175.7 4.2 %gather_fusion.1 = f32[32,5,3,6,6]{4,3,2,1,0:T(8,128)} fusion(f32[64,5,3,6,6]{4,3,2,1,0:T(8,128)} %bitcast.214, s32[1024]{0:T(1024)} %get-tuple-element.249), kind=kCustom, calls=%fused_computation.1 | custom fusion | bytes 138368 | tf_op jit(solution)/shard_map/gather | solution.py:209
  186.5 3.2 %copy.1295 = f32[32,5,2,16,16]{4,3,2,1,0:T(8,128)} copy(f32[32,5,2,16,16]{0,4,3,2,1:T(8,128)} %add_bitcast_fusion) | data formatting | bytes 655360 | tf_op jit(solution)/shard_map/transpose | solution.py:150
  199.6 5.6 %multiply_subtract_fusion = (f32[5,32,16,128]{3,2,1,0:T(8,128)S(1)}, f32[5,32,16,128]{3,2,1,0:T(8,128)S(1)}, f32[5,32,16,128]{3,2,1,0:T(8,128)S(1)}, f32[5,32,16...) fusion(f32[5,32,16,128]{3,2,1,0:T(8,128)S(1)} %constant_dynamic-update-slice_fusion, ...), kind=kLoop, calls=%fused_computation.31 | loop fusion | flops 15073280 | bytes 17039360 | tf_op jit(solution)/shard_map/sub | solution.py:103
  214.9 2.8 fusion.44
  225.0 2.2 stack.130
  241.9 2.2 stack.136
  271.6 3.9 %fusion.1 = f32[5,2,4,8,4]{4,3,2,1,0:T(8,128)S(1)} fusion(f32[5,2,1,4,4,8,1,4,4]{8,7,5,4,3,1,6,2,0:T(4,128)S(1)} %constant_dynamic-update-slice_fusion.136, f32[5,2,1,4,4,8,1,4,4]{8,7,5,4,3,1,6,2,0:T(4,128)S(1)} %constant_dynamic-update-slice_fusion.141, f32[5,2,1,4,4,8,1,4,4]{8,7,5,4,3,1,6,2,0:T(4,128)S(1)} %constant_dynamic-update-slice_fusion.131, ...), kind=kLoop, calls=%fused_computation.5 | loop fusion | flops 162560 | bytes 398336 | tf_op jit(solution)/shard_map/reduce_sum | solution.py:161
  275.5 4.9 %reshape_squeeze.4 = f32[5,2,4,4,8,4,4]{6,5,4,3,2,1,0:T(4,128)} reshape(f32[5,32,128]{2,1,0:T(8,128)S(1)} %slice_reduce_fusion) | data formatting | bytes 163840 | tf_op jit(solution)/shard_map/reshape;squeeze | solution.py:160
  280.4 2.4 reduce_sum.41
  284.3 4.5 %all-to-all-start.2 = ((f32[8,8,80]{2,1,0:T(8,128)}), f32[8,8,80]{2,1,0:T(8,128)S(1)}, u32[]{:S(2)}, u32[]{:S(2)}) async-start(f32[8,8,80]{2,1,0:T(8,128)} %fusion.26), calls=%async_computation.2 | async-start | bytes 65536 | tf_op jit(solution)/shard_map/all_to_all | solution.py:225
  295.6 4.1 %copy.1320 = f32[5,32,128,16]{1,3,2,0:T(8,128)} copy(f32[5,32,128,16]{2,3,1,0:T(8,128)S(1)} %fusion.7) | data formatting | bytes 2621440 | tf_op jit(solution)/shard_map/transpose | solution.py:215
  299.6 5.0 %copy.1323 = f32[5,32,2048]{2,1,0:T(8,128)} copy(f32[5,32,2048]{1,2,0:T(8,128)} %bitcast.209) | data formatting | bytes 2621440
  (439 shorter events, 182.1 us)
Async XLA Ops:
  0.6 47.2 %copy-start = (f32[128,5,512]{2,0,1:T(8,128)S(1)}, f32[128,5,512]{2,0,1:T(8,128)}, u32[]{:S(2)}) copy-start(f32[128,5,512]{2,0,1:T(8,128)} %param.5) | copy-start | bytes 3932164
  3.0 11.2 %copy-start.83 = (s32[32]{0:T(128)}, s32[32]{0:T(128)S(1)}, u32[]{:S(2)}) copy-start(s32[32]{0:T(128)S(1)} %get-tuple-element.239) | copy-start | bytes 388
  4.5 42.6 %all-to-all-start = ((s32[8,1,8]{2,1,0:T(1,128)}), s32[8,1,8]{2,1,0:T(1,128)S(1)}, u32[]{:S(2)}, u32[]{:S(2)}) async-start(s32[8,1,8]{2,1,0:T(1,128)} %bitcast.25), calls=%async_computation | async-start | bytes 8192 | tf_op jit(solution)/shard_map/all_to_all | solution.py:201
  22.6 141.9 %collective-permute-start.2 = (f32[5,2,16,128]{3,2,1,0:T(8,128)}, f32[5,2,16,128]{3,2,1,0:T(8,128)}, u32[]{:S(2)}, u32[]{:S(2)}) collective-permute-start(f32[5,2,16,128]{3,2,1,0:T(8,128)} %get-tuple-element.146), channel_id=1, source_target_pairs={{0,8},{8,16},{16,24},{24,0},{1,9},{9,17},{17,25},{25,1},{2,10},{10... | collective-permute-start | bytes 245768 | tf_op jit(solution)/shard_map/ppermute | solution.py:27
  24.2 141.1 %collective-permute-start.3 = (f32[5,2,16,128]{3,2,1,0:T(8,128)}, f32[5,2,16,128]{3,2,1,0:T(8,128)}, u32[]{:S(2)}, u32[]{:S(2)}) collective-permute-start(f32[5,2,16,128]{3,2,1,0:T(8,128)} %get-tuple-element.147), channel_id=1, source_target_pairs={{8,0},{16,8},{24,16},{0,24},{9,1},{17,9},{25,17},{1,25},{10,2},{18... | collective-permute-start | bytes 245768 | tf_op jit(solution)/shard_map/ppermute | solution.py:30
  30.9 46.7 %collective-permute-start = (f32[5,32,16,2]{1,2,3,0:T(8,128)}, f32[5,32,16,2]{1,2,3,0:T(8,128)}, u32[]{:S(2)}, u32[]{:S(2)}) collective-permute-start(f32[5,32,16,2]{1,2,3,0:T(8,128)} %copy.1220), channel_id=1, source_target_pairs={{0,1},{1,2},{2,3},{3,4},{4,5},{5,6},{6,7},{8,9},{9,10},{10,11},{11... | collective-permute-start | bytes 61448 | tf_op jit(solution)/shard_map/ppermute | solution.py:27
  35.3 48.5 %collective-permute-start.1 = (f32[5,32,16,2]{1,2,3,0:T(8,128)S(1)}, f32[5,32,16,2]{1,2,3,0:T(8,128)}, u32[]{:S(2)}, u32[]{:S(2)}) collective-permute-start(f32[5,32,16,2]{1,2,3,0:T(8,128)S(1)} %copy.1222), channel_id=1, source_target_pairs={{1,0},{2,1},{3,2},{4,3},{5,4},{6,5},{7,6},{9,8},{10,9},{11,10},{12... | collective-permute-start | bytes 61448 | tf_op jit(solution)/shard_map/ppermute | solution.py:30
  36.8 9.6 %copy-start.77 = (f32[4]{0:T(128)}, f32[4]{0:T(128)S(1)}, u32[]{:S(2)}) copy-start(f32[4]{0:T(128)S(1)} %multiply_add_fusion.20) | copy-start | bytes 52
  69.6 96.9 %all-to-all-start.1 = ((f32[8,1,4320]{2,1,0:T(1,128)}), f32[8,1,4320]{2,1,0:T(1,128)S(1)}, u32[]{:S(2)}, u32[]{:S(2)}) async-start(f32[8,1,4320]{2,1,0:T(1,128)} %reshape.2270), calls=%async_computation.1 | async-start | bytes 278528 | tf_op jit(solution)/shard_map/all_to_all | solution.py:207
  107.2 12.4 %copy-start.43 = (f32[1,32,16,1]{3,2,1,0:T(8,128)S(1)}, f32[1,32,16,1]{3,2,1,0:T(8,128)}, u32[]{:S(2)}) copy-start(f32[1,32,16,1]{3,2,1,0:T(8,128)} %get-tuple-element.159) | copy-start | bytes 6148
  108.9 11.4 %copy-start.42 = (f32[1,32,16,1]{3,2,1,0:T(8,128)S(1)}, f32[1,32,16,1]{3,2,1,0:T(8,128)}, u32[]{:S(2)}) copy-start(f32[1,32,16,1]{3,2,1,0:T(8,128)} %get-tuple-element.161) | copy-start | bytes 6148
  110.1 10.2 %copy-start.44 = (f32[1,32,16,1]{1,2,3,0:T(8,128)}, f32[1,32,16,1]{1,2,3,0:T(8,128)S(1)}, u32[]{:S(2)}) copy-start(f32[1,32,16,1]{1,2,3,0:T(8,128)S(1)} %copy.1233) | copy-start | bytes 6148
  126.9 19.0 %copy-start.41 = (f32[1,32,16,1]{3,2,1,0:T(8,128)S(1)}, f32[1,32,16,1]{3,2,1,0:T(8,128)}, u32[]{:S(2)}) copy-start(f32[1,32,16,1]{3,2,1,0:T(8,128)} %get-tuple-element.158) | copy-start | bytes 6148
  126.9 19.7 %copy-start.40 = (f32[1,32,16,1]{3,2,1,0:T(8,128)S(1)}, f32[1,32,16,1]{3,2,1,0:T(8,128)}, u32[]{:S(2)}) copy-start(f32[1,32,16,1]{3,2,1,0:T(8,128)} %get-tuple-element.160) | copy-start | bytes 6148
  214.1 3.7 %copy-start.58 = (f32[1,32,1,128]{3,2,1,0:T(1,128)S(1)}, f32[1,32,1,128]{3,2,1,0:T(1,128)}, u32[]{:S(2)}) copy-start(f32[1,32,1,128]{3,2,1,0:T(1,128)} %get-tuple-element.203) | copy-start | bytes 49156
  217.8 9.5 %copy-start.56 = (f32[32,128]{1,0:T(8,128)S(1)}, f32[32,128]{1,0:T(8,128)}, u32[]{:S(2)}) copy-start(f32[32,128]{1,0:T(8,128)} %get-tuple-element.198) | copy-start | bytes 49156
  218.5 10.2 %copy-start.55 = (f32[32,128]{1,0:T(8,128)S(1)}, f32[32,128]{1,0:T(8,128)}, u32[]{:S(2)}) copy-start(f32[32,128]{1,0:T(8,128)} %get-tuple-element.195) | copy-start | bytes 49156
  221.5 8.8 %copy-start.57 = (f32[32,128]{1,0:T(8,128)S(1)}, f32[32,128]{1,0:T(8,128)}, u32[]{:S(2)}) copy-start(f32[32,128]{1,0:T(8,128)} %get-tuple-element.188) | copy-start | bytes 49156
  224.4 7.4 %copy-start.68 = (f32[32,128]{1,0:T(8,128)S(1)}, f32[32,128]{1,0:T(8,128)}, u32[]{:S(2)}) copy-start(f32[32,128]{1,0:T(8,128)} %get-tuple-element.185) | copy-start | bytes 49156
  228.7 6.4 %copy-start.67 = (f32[1,32,1,128]{3,2,1,0:T(1,128)S(1)}, f32[1,32,1,128]{3,2,1,0:T(1,128)}, u32[]{:S(2)}) copy-start(f32[1,32,1,128]{3,2,1,0:T(1,128)} %get-tuple-element.209) | copy-start | bytes 49156
  230.2 7.2 %copy-start.66 = (f32[1,32,1,128]{3,2,1,0:T(1,128)S(1)}, f32[1,32,1,128]{3,2,1,0:T(1,128)}, u32[]{:S(2)}) copy-start(f32[1,32,1,128]{3,2,1,0:T(1,128)} %get-tuple-element.206) | copy-start | bytes 49156
  235.2 9.0 %copy-start.65 = (f32[32,128]{1,0:T(8,128)S(1)}, f32[32,128]{1,0:T(8,128)}, u32[]{:S(2)}) copy-start(f32[32,128]{1,0:T(8,128)} %get-tuple-element.204) | copy-start | bytes 49156
  235.9 9.7 %copy-start.64 = (f32[32,128]{1,0:T(8,128)S(1)}, f32[32,128]{1,0:T(8,128)}, u32[]{:S(2)}) copy-start(f32[32,128]{1,0:T(8,128)} %get-tuple-element.49) | copy-start | bytes 49156
  238.2 9.0 %copy-start.54 = (f32[32,128]{1,0:T(8,128)S(1)}, f32[32,128]{1,0:T(8,128)}, u32[]{:S(2)}) copy-start(f32[32,128]{1,0:T(8,128)} %get-tuple-element.191) | copy-start | bytes 49156
  240.4 8.2 %copy-start.48 = (f32[5,32,1,128]{3,2,1,0:T(1,128)S(1)}, f32[5,32,1,128]{3,2,1,0:T(1,128)}, u32[]{:S(2)}) copy-start(f32[5,32,1,128]{3,2,1,0:T(1,128)} %copy-done.47) | copy-start | bytes 245764
  240.4 8.2 %copy-start.53 = (f32[1,32,1,128]{3,2,1,0:T(1,128)S(1)}, f32[1,32,1,128]{3,2,1,0:T(1,128)}, u32[]{:S(2)}) copy-start(f32[1,32,1,128]{3,2,1,0:T(1,128)} %get-tuple-element.190) | copy-start | bytes 49156
  248.6 8.8 %copy-start.52 = (f32[32,128]{1,0:T(8,128)S(1)}, f32[32,128]{1,0:T(8,128)}, u32[]{:S(2)}) copy-start(f32[32,128]{1,0:T(8,128)} %get-tuple-element.28) | copy-start | bytes 49156
  249.4 9.8 %copy-start.51 = (f32[32,128]{1,0:T(8,128)S(1)}, f32[32,128]{1,0:T(8,128)}, u32[]{:S(2)}) copy-start(f32[32,128]{1,0:T(8,128)} %get-tuple-element.24) | copy-start | bytes 49156
  284.3 20.3 %all-to-all-start.2 = ((f32[8,8,80]{2,1,0:T(8,128)}), f32[8,8,80]{2,1,0:T(8,128)S(1)}, u32[]{:S(2)}, u32[]{:S(2)}) async-start(f32[8,8,80]{2,1,0:T(8,128)} %fusion.26), calls=%async_computation.2 | async-start | bytes 65536 | tf_op jit(solution)/shard_map/all_to_all | solution.py:225
  299.6 5.1 %copy-start.81 = (s32[64]{0:T(128)S(1)}, s32[64]{0:T(128)}, u32[]{:S(2)}) copy-start(s32[64]{0:T(128)} %eq.129) | copy-start | bytes 772
  299.6 5.1 %copy-start.82 = (s32[2,128]{1,0:T(2,128)S(1)}, s32[2,128]{1,0:T(2,128)}, u32[]{:S(2)}) copy-start(s32[2,128]{1,0:T(2,128)} %multiply_add_fusion.19) | copy-start | bytes 3076
  299.6 6.0 %copy-start.1 = (f32[128,5,512]{2,0,1:T(8,128)S(1)}, f32[128,5,512]{2,0,1:T(8,128)}, u32[]{:S(2)}) copy-start(f32[128,5,512]{2,0,1:T(8,128)} %param.5) | copy-start | bytes 3932164
  (60 other events, 98.9 us)
where the time goes:
time: 312 us; the launch traced here: 306 us
  local copies, waits for them, and re-layouts  199 us (64%)
  other arithmetic  79.2 us (25%)
  starting transfers between devices  23.6 us (8%)
    unnamed x206, local copies, waits for them, and re-layouts  46.4 us
    unnamed x53, other arithmetic  23.2 us
    another operation x14, local copies, waits for them, and re-layouts, state_terms(): jnp.stack(flux_list)  15.7 us
    another operation x20, local copies, waits for them, and re-layouts, state_terms(): jnp.stack(cons_list)  13.8 us
    slice x12, local copies, waits for them, and re-layouts, part_of(): return lax.slice_in_dim(array, start, stop, axis=dim_index)  12.8 us
    sub x2, other arithmetic, face_fluxes(): primitive - 0.5 * slopes  9.46 us
    reshape x4, local copies, waits for them, and re-layouts, assemble(): chosen.transpose(4, 0, 3, 6, 5, 1, 2, 7)  7.64 us
    reshape x1, local copies, waits for them, and re-layouts, extract(): shaped = box_cells.reshape(box_cells.shape[:-1] + (CB, CB, CB))  7.42 us
  transfers between devices with their start and end apart: 7, of which 0 were waited for; matrix products, arithmetic and copies ran while one was open for 50% of the time, Pallas kernels for 0%

commit v1 on v0

v1 whole, which is shorter than its diff:
```python
import functools

import jax
import jax.numpy as jnp
from jax import lax
from jax.experimental import pallas as pl
from jax.experimental.pallas import tpu as pltpu
from jax.sharding import PartitionSpec as P

PS = 16
RATIO = 4
QS = 16
CF = 4
CB = 8
NF = 5
LANES = 128
ROWS = 8
SIDES = 2
QUANT = 4

GAMMA = 1.4
DT_DX = 0.08
OFFSETS = [(i + 0.5) / RATIO - 0.5 for i in range(RATIO)]
F32, BF16, I32 = jnp.float32, jnp.bfloat16, jnp.int32
TABLE_ROWS = NF * QUANT * CF * CF
TABLE_PAD = 384
TERM_ROWS = 32


def iota(shape, dim):
    return lax.broadcasted_iota(I32, shape, dim)


def minmod(a, b):
    return jnp.maximum(jnp.minimum(a, b), 0.0) + jnp.minimum(jnp.maximum(a, b), 0.0)


def to_primitive(cons):
    inverse = 1.0 / cons[0]
    velocity = [cons[1 + i] * inverse for i in range(3)]
    kinetic = cons[1] * velocity[0] + cons[2] * velocity[1] + cons[3] * velocity[2]
    return [cons[0]] + velocity + [(GAMMA - 1.0) * (cons[4] - 0.5 * kinetic)]


def hll(low, up, normal):
    others = [1 + i for i in range(3) if i != normal]
    u_low, u_up = low[1 + normal], up[1 + normal]
    p_low, p_up = low[4], up[4]
    g_low, g_up = GAMMA * p_low, GAMMA * p_up
    c_low = g_low * lax.rsqrt(g_low * low[0])
    c_up = g_up * lax.rsqrt(g_up * up[0])
    slow = jnp.minimum(jnp.minimum(u_low - c_low, u_up - c_up), 0.0)
    fast = jnp.maximum(jnp.maximum(u_low + c_low, u_up + c_up), 0.0)
    inverse = 1.0 / (fast - slow)
    f = fast * inverse
    s = slow * inverse
    a = f * (u_low - slow)
    b = s * (u_up - fast)
    m_low = a * low[0]
    m_up = b * up[0]
    k_low = 0.5 * (low[1] * low[1] + low[2] * low[2] + low[3] * low[3])
    k_up = 0.5 * (up[1] * up[1] + up[2] * up[2] + up[3] * up[3])
    rest = 1.0 / (GAMMA - 1.0)
    flux = [m_low - m_up, None, None, None, None]
    for i in others:
        flux[i] = m_low * low[i] - m_up * up[i]
    flux[1 + normal] = (m_low * u_low + f * p_low) - (m_up * u_up + s * p_up)
    flux[4] = (m_low * k_low + p_low * (rest * a + f * u_low)) - (
        m_up * k_up + p_up * (rest * b + s * u_up)
    )
    return flux


def split3(x):
    high = x.astype(BF16)
    left = x - high.astype(F32)
    middle = left.astype(BF16)
    low = (left - middle.astype(F32)).astype(BF16)
    return [high, middle, low]


def swap_groups(tiles, lane):
    tiles = list(tiles)
    bit = 0
    while (1 << bit) < len(tiles):
        step = 1 << bit
        upper = ((lane >> bit) & 1) == 1
        for i in range(len(tiles)):
            if not i & step:
                first, second = tiles[i], tiles[i + step]
                tiles[i] = jnp.where(upper, pltpu.roll(second, step, 1), first)
                tiles[i + step] = jnp.where(upper, second, pltpu.roll(first, LANES - step, 1))
        bit += 1
    return tiles


def count_slots(owner_ref, count_ref, members, capacity, pieces):
    for m in range(members):
        count_ref[m] = 0
    slots = []
    for p in range(pieces):
        owner = owner_ref[p, 0]
        rank = count_ref[owner]
        count_ref[owner] = rank + 1
        slots.append(owner * capacity + rank)
    return slots


def prep_kernel(members, capacity, boxes, owner_ref, box_ref, fine_ref, msg_ref, lo_ref, hi_ref, count_ref):
    me = lax.axis_index("dev")
    pieces = box_ref.shape[0]
    chunks = fine_ref.shape[2] // LANES
    blocks = fine_ref.shape[1] // ROWS
    lane = iota((ROWS, LANES), 1)
    sub = iota((ROWS, LANES), 0)
    slots = count_slots(owner_ref, count_ref, members, capacity, pieces)
    values = jnp.zeros((ROWS, LANES), I32)
    for p in range(pieces):
        values = jnp.where(lane == slots[p], box_ref[p] + (boxes * (p % SIDES) + 1), values)
    values = jnp.where(sub == 0, values, 0).astype(F32)
    mine = (lane >= me * capacity) & (lane < (me + 1) * capacity)
    for m in range(members):
        shift = lax.rem((me - m) * capacity + LANES * members, LANES)
        msg_ref[m, NF * ROWS :, :] = jnp.where(mine, pltpu.roll(values, shift, 1), 0.0)
    width = 2 * PS
    for f in range(NF):
        left = fine_ref[f, 0:ROWS, 0:LANES]
        right = pltpu.roll(fine_ref[f, 0:ROWS, (chunks - 1) * LANES :], width, 1)
        for g in range(1, blocks):
            rows = slice(g * ROWS, (g + 1) * ROWS)
            here = lane // width == g
            left = jnp.where(here, pltpu.roll(fine_ref[f, rows, 0:LANES], width * g, 1), left)
            edge = fine_ref[f, rows, (chunks - 1) * LANES :]
            shift = (width * (g + 1)) % LANES
            right = jnp.where(here, pltpu.roll(edge, shift, 1) if shift else edge, right)
        for m in range(members):
            below = jnp.full((ROWS, LANES), m, I32) < me
            msg_ref[m, f * ROWS : (f + 1) * ROWS, :] = jnp.where(below, left, right)
    for f in range(NF):
        for j in range(chunks // 4):
            low = high = None
            for k in range(4):
                c = slice((4 * j + k) * LANES, (4 * j + k + 1) * LANES)
                first = fine_ref[f, 0:ROWS, c]
                last = fine_ref[f, (blocks - 1) * ROWS :, c]
                first = pltpu.roll(first, 2 * k, 0) if k else first
                last = pltpu.roll(last, 2 * k + 2, 0) if k < 3 else last
                low = first if k == 0 else jnp.where(sub // 2 == k, first, low)
                high = last if k == 0 else jnp.where(sub // 2 == k, last, high)
            lo_ref[f, j * ROWS : (j + 1) * ROWS, :] = low
            hi_ref[f, j * ROWS : (j + 1) * ROWS, :] = high


def build_kernel(
    members, capacity, owner_ref, fine_ref, coarse_ref,
    wn_ref, wz_ref, zc_ref, tab_ref, he_ref,
    count_ref, ct_ref,
):
    lane = iota((ROWS, LANES), 1)
    sub = iota((ROWS, LANES), 0)
    chunks = fine_ref.shape[2] // LANES
    blocks = fine_ref.shape[1] // ROWS
    patch_y = fine_ref.shape[1] // PS
    patch_x = chunks * LANES // PS // PS
    pieces = owner_ref.shape[0]
    slot_count = members * capacity

    def primitive_block(block, carry):
        rows = pl.ds(pl.multiple_of(block * ROWS, ROWS), ROWS)
        for c in range(chunks):
            prim = to_primitive(
                [fine_ref[f, rows, c * LANES : (c + 1) * LANES] for f in range(NF)]
            )
            for f in range(NF):
                wn_ref[f, c, rows, :] = prim[f]
        return carry

    lax.fori_loop(0, blocks, primitive_block, 0)

    def turn(step, carry):
        f = step // blocks
        rows = pl.ds(pl.multiple_of((step % blocks) * ROWS, ROWS), ROWS)
        tiles = swap_groups([wn_ref[f, c, rows, :] for c in range(chunks)], lane)
        for z in range(PS):
            wz_ref[f, z, rows, :] = tiles[z]
        return carry

    lax.fori_loop(0, NF * blocks, turn, 0)

    def sweep(block, carry):
        rows = pl.ds(pl.multiple_of(block * ROWS, ROWS), ROWS)

        def load(z):
            return [wz_ref[f, z, rows, :] for f in range(NF)]

        w_here = load(1)
        w_before = load(0)
        diff = [w_here[f] - w_before[f] for f in range(NF)]
        low = flux = None
        for z in range(1, PS - 1):
            w_next = load(z + 1)
            diff_next = [w_next[f] - w_here[f] for f in range(NF)]
            half = [0.5 * minmod(diff[f], diff_next[f]) for f in range(NF)]
            if z >= 2:
                new = hll(low, [w_here[f] - half[f] for f in range(NF)], 2)
                for f in range(NF):
                    zc_ref[f, z - 2, rows, :] = new[f] if z == 2 else new[f] - flux[f]
                flux = new
            low = [w_here[f] + half[f] for f in range(NF)]
            w_here, diff = w_next, diff_next
        for f in range(NF):
            zc_ref[f, PS - 3, rows, :] = -flux[f]
        return carry

    lax.fori_loop(0, blocks, sweep, 0)

    slots = count_slots(owner_ref, count_ref, members, capacity, pieces)
    x_cell = (lane % PS) * (LANES // PS) + lane // PS
    for s in range(SIDES):
        for ky in range(patch_y):
            code = jnp.zeros((ROWS, LANES), I32)
            for kx in range(patch_x):
                slot = slots[(ky * patch_x + kx) * SIDES + s]
                code = jnp.where(x_cell // PS == kx, slot, code)
            code = code + (x_cell // RATIO) % CF * slot_count
            at = (s * patch_y + ky) * LANES
            hot = iota((CF * slot_count, LANES), 0) == code[0:1, :]
            he_ref[:, at : at + LANES] = jnp.where(hot, 1.0, 0.0).astype(BF16)

    boxes = coarse_ref.shape[0]
    for f in range(NF):
        for j in range(CB * CB * CB // LANES):
            at = slice(j * LANES, (j + 1) * LANES)
            ct_ref[f, at, :] = coarse_ref[:, f, at].T
    tab_ref[:, TABLE_ROWS:, :] = jnp.zeros((3, TABLE_PAD - TABLE_ROWS, SIDES * boxes), BF16)
    for s in range(SIDES):
        middle = CB - 3 if s == 0 else 2

        def cells(z, y):
            at = (z * CB + y) * CB
            return to_primitive([ct_ref[f, at : at + CB, :] for f in range(NF)])

        centre = {y: cells(middle, y) for y in range(1, CB - 1)}
        found = {}
        for cy in range(CF):
            y = cy + 2
            below, above = cells(middle - 1, y), cells(middle + 1, y)
            for f in range(NF):
                c = centre[y][f]
                found[f, 0, cy] = c
                found[f, 1, cy] = minmod(c - below[f], above[f] - c)
                found[f, 2, cy] = minmod(c - centre[y - 1][f], centre[y + 1][f] - c)
                found[f, 3, cy] = minmod(c - pltpu.roll(c, 1, 0), pltpu.roll(c, ROWS - 1, 0) - c)
        for f in range(NF):
            for q in range(QUANT):
                halves = [
                    jnp.where(
                        sub < CF,
                        pltpu.roll(found[f, q, 2 * i], ROWS - 2, 0),
                        pltpu.roll(found[f, q, 2 * i + 1], 2, 0),
                    )
                    for i in range(2)
                ]
                tile = jnp.concatenate(halves, axis=0)
                at = (f * QUANT + q) * CF * CF
                for number, part in enumerate(split3(tile)):
                    tab_ref[number, at : at + CF * CF, s * boxes : (s + 1) * boxes] = part


def serve_kernel(msg_ref, tab_ref, out_ref, hot_ref):
    members = msg_ref.shape[0]
    slot_count = out_ref.shape[0]
    row = msg_ref[0, NF * ROWS :, :]
    for m in range(1, members):
        row = row + msg_ref[m, NF * ROWS :, :]
    shape = (slot_count, LANES)
    wide = jnp.broadcast_to(row[0:1, :], shape)
    column = jnp.sum(jnp.where(iota(shape, 0) == iota(shape, 1), wide, 0.0), axis=1, keepdims=True)
    target = column.astype(I32) - 1
    hot = jnp.where(iota(hot_ref.shape, 1) == target, 1.0, 0.0).astype(BF16)
    hot_ref[...] = hot
    total = None
    for part in range(3):
        got = lax.dot_general(
            hot, tab_ref[part], (((1,), (1,)), ((), ())), preferred_element_type=F32
        )
        total = got if total is None else total + got
    out_ref[...] = total


def sweep_line(tiles, normal, back, forward, emit):
    fields = range(NF)
    last = len(tiles) - 1

    def join_back(before, here):
        return [back(before[f], here[f]) for f in fields]

    moved = [[back(None, t[f]) for f in fields] for t in tiles]
    diff = [
        [t[f] - back(moved[max(i - 1, 0)][f], moved[i][f]) for f in fields]
        for i, t in enumerate(tiles)
    ]
    diff_moved = [[forward(None, d[f]) for f in fields] for d in diff]
    low_moved = None
    flux = flux_moved = None
    for i, t in enumerate(tiles):
        half = [
            0.5 * minmod(diff[i][f], forward(diff_moved[i][f], diff_moved[min(i + 1, last)][f]))
            for f in fields
        ]
        low_next = [back(None, t[f] + half[f]) for f in fields]
        if i > 0:
            left = [back(low_moved[f], low_next[f]) for f in fields]
            new = hll(left, [t[f] - half[f] for f in fields], normal)
            new_moved = [forward(None, new[f]) for f in fields]
            if i > 1:
                emit(i - 2, [forward(flux_moved[f], new_moved[f]) - flux[f] for f in fields])
            flux, flux_moved = new, new_moved
        low_moved = low_next


def plane_kernel(members, msg_ref, lo_ref, hi_ref, wn_ref, out_ref):
    me = lax.axis_index("dev")
    chunks = wn_ref.shape[1]
    blocks = wn_ref.shape[2] // ROWS
    lane = iota((ROWS, LANES), 1)
    sub = iota((ROWS, LANES), 0)
    width = 2 * PS
    place = jnp.full((ROWS, LANES), me, I32)

    def x_back(before, here):
        if before is None:
            return pltpu.roll(here, PS, 1)
        return jnp.where(lane < PS, before, here)

    def x_forward(here, after):
        if here is None:
            return pltpu.roll(after, LANES - PS, 1)
        return jnp.where(lane >= LANES - PS, after, here)

    def x_block(block, carry):
        rows = pl.ds(pl.multiple_of(block * ROWS, ROWS), ROWS)
        left = jnp.maximum(me - 1, 0)
        right = jnp.minimum(me + 1, members - 1)
        shift_low = lax.rem(2 * LANES - width - width * block, LANES)
        shift_high = lax.rem(LANES - width * block, LANES)
        low = to_primitive(
            [pltpu.roll(msg_ref[left, f * ROWS : (f + 1) * ROWS, :], shift_low, 1) for f in range(NF)]
        )
        high = to_primitive(
            [pltpu.roll(msg_ref[right, f * ROWS : (f + 1) * ROWS, :], shift_high, 1) for f in range(NF)]
        )
        tiles = [[wn_ref[f, c, rows, :] for f in range(NF)] for c in range(chunks)]
        for f in range(NF):
            w = tiles[0][f]
            same = jnp.where(
                lane < LANES - PS, pltpu.roll(w, LANES - width, 1), pltpu.roll(w, LANES - PS, 1)
            )
            low[f] = jnp.where(place == 0, same, low[f])
            w = tiles[-1][f]
            same = jnp.where(lane < PS, pltpu.roll(w, PS, 1), pltpu.roll(w, width, 1))
            high[f] = jnp.where(place == members - 1, same, high[f])

        def emit(c, change):
            for f in range(NF):
                out_ref[f, c, rows, :] = change[f]

        sweep_line([low] + tiles + [high], 0, x_back, x_forward, emit)
        return carry

    lax.fori_loop(0, blocks, x_block, 0)

    def y_back(before, here):
        if before is None:
            return pltpu.roll(here, 1, 0)
        return jnp.where(sub < 1, before, here)

    def y_forward(here, after):
        if here is None:
            return pltpu.roll(after, ROWS - 1, 0)
        return jnp.where(sub >= ROWS - 1, after, here)

    def y_block(j, carry):
        rows = pl.ds(pl.multiple_of(j * ROWS, ROWS), ROWS)
        low = to_primitive([lo_ref[f, rows, :] for f in range(NF)])
        high = to_primitive([hi_ref[f, rows, :] for f in range(NF)])
        for k in range(4):
            c = 4 * j + k
            below = [pltpu.roll(t, (ROWS - 2 - 2 * k) % ROWS, 0) if k < 3 else t for t in low]
            above = [pltpu.roll(t, ROWS - 2 * k, 0) if k else t for t in high]
            tiles = [
                [wn_ref[f, c, b * ROWS : (b + 1) * ROWS, :] for f in range(NF)]
                for b in range(blocks)
            ]

            def emit(b, change):
                at = slice(b * ROWS, (b + 1) * ROWS)
                for f in range(NF):
                    out_ref[f, c, at, :] = out_ref[f, c, at, :] + change[f]

            sweep_line([below] + tiles + [above], 1, y_back, y_forward, emit)
        return carry

    lax.fori_loop(0, chunks // 4, y_block, 0)


def face_kernel(
    slot_count, got_ref, he_ref, wz_ref, zc_ref, term_ref, edge_ref,
    rt_ref, lf_ref, g_ref, fs_ref, v_ref,
):
    lane = iota((ROWS, LANES), 1)
    sub = iota((ROWS, LANES), 0)
    rows_all = NF * QUANT * CF
    y_cells = wz_ref.shape[2]
    blocks = y_cells // ROWS
    patch_y = y_cells // PS
    rt_ref[...] = got_ref[...].T
    for cx in range(CF):
        lf_ref[:, cx * slot_count : (cx + 1) * slot_count] = rt_ref[
            pl.ds(cx, rows_all, stride=CF), :
        ]
    parts = jnp.concatenate(split3(lf_ref[...]), axis=0)
    product = jnp.dot(parts, he_ref[...], preferred_element_type=F32)
    g_ref[...] = (
        product[0:rows_all] + product[rows_all : 2 * rows_all] + product[2 * rows_all :]
    )

    def pick(options, index):
        value = jnp.full((ROWS, LANES), options[0], F32)
        for i in range(1, RATIO):
            value = jnp.where(index == i, options[i], value)
        return value

    off_y = pick(OFFSETS, sub % RATIO)
    off_x = pick(OFFSETS, (lane // PS) % RATIO)
    for block in range(blocks):
        ky, half = block // (blocks // patch_y), block % (blocks // patch_y)
        rows = slice(block * ROWS, (block + 1) * ROWS)
        for s in range(SIDES):
            at = (s * patch_y + ky) * LANES
            ghosts = [[], []]
            for f in range(NF):
                terms = []
                for q in range(QUANT):
                    r = (f * QUANT + q) * CF + 2 * half
                    terms.append(
                        jnp.where(
                            sub < RATIO,
                            jnp.broadcast_to(g_ref[r : r + 1, at : at + LANES], (ROWS, LANES)),
                            jnp.broadcast_to(g_ref[r + 1 : r + 2, at : at + LANES], (ROWS, LANES)),
                        )
                    )
                for i in range(2):
                    off_z = OFFSETS[i + (RATIO - 2 if s == 0 else 0)]
                    ghosts[i].append(
                        ((terms[0] + terms[1] * off_z) + terms[2] * off_y) + terms[3] * off_x
                    )

            def load(z):
                return [wz_ref[f, z, rows, :] for f in range(NF)]

            if s == 0:
                line = ghosts + [load(0), load(1), load(2)]
            else:
                line = [load(PS - 3), load(PS - 2), load(PS - 1)] + ghosts
            diff = [[line[i + 1][f] - line[i][f] for f in range(NF)] for i in range(4)]
            half_slope = [
                [0.5 * minmod(diff[i][f], diff[i + 1][f]) for f in range(NF)] for i in range(3)
            ]
            flux = [
                hll(
                    [line[i + 1][f] + half_slope[i][f] for f in range(NF)],
                    [line[i + 2][f] - half_slope[i + 1][f] for f in range(NF)],
                    2,
                )
                for i in range(2)
            ]
            for f in range(NF):
                if s == 0:
                    edge_ref[f, 0, rows, :] = flux[1][f] - flux[0][f]
                    edge_ref[f, 1, rows, :] = zc_ref[f, 0, rows, :] - flux[1][f]
                    fs_ref[0, f, rows, :] = flux[0][f]
                else:
                    edge_ref[f, 2, rows, :] = zc_ref[f, PS - 3, rows, :] + flux[0][f]
                    edge_ref[f, 3, rows, :] = flux[1][f] - flux[0][f]
                    fs_ref[1, f, rows, :] = flux[1][f]

    v_ref[NF * CF :, :] = jnp.zeros((TERM_ROWS - NF * CF, v_ref.shape[1]), F32)
    for s in range(SIDES):
        for f in range(NF):
            total = None
            for i in range(RATIO):
                got = fs_ref[s, f, pl.ds(i, y_cells // RATIO, stride=RATIO), :]
                total = got if total is None else total + got
            total = total * (1.0 / RATIO)
            for ky in range(patch_y):
                at = (s * patch_y + ky) * LANES
                v_ref[f * CF : (f + 1) * CF, at : at + LANES] = total[ky * CF : (ky + 1) * CF]
    parts = jnp.concatenate(split3(v_ref[...]), axis=0)
    product = lax.dot_general(
        parts, he_ref[...], (((1,), (1,)), ((), ())), preferred_element_type=F32
    )
    summed = (
        product[0:TERM_ROWS] + product[TERM_ROWS : 2 * TERM_ROWS] + product[2 * TERM_ROWS :]
    )
    turned = summed.T
    for cx in range(CF):
        term_ref[:, cx * TERM_ROWS : (cx + 1) * TERM_ROWS] = turned[
            cx * slot_count : (cx + 1) * slot_count, :
        ]


def final_kernel(fine_ref, plane_ref, zc_ref, edge_ref, out_ref):
    lane = iota((ROWS, LANES), 1)
    chunks = plane_ref.shape[1]
    blocks = plane_ref.shape[2] // ROWS

    def turn(step, carry):
        f = step // blocks
        rows = pl.ds(pl.multiple_of((step % blocks) * ROWS, ROWS), ROWS)
        tiles = [edge_ref[f, 0, rows, :], edge_ref[f, 1, rows, :]]
        tiles += [zc_ref[f, z - 1, rows, :] for z in range(2, PS - 2)]
        tiles += [edge_ref[f, 2, rows, :], edge_ref[f, 3, rows, :]]
        tiles = swap_groups(tiles, lane)
        for c in range(chunks):
            at = slice(c * LANES, (c + 1) * LANES)
            change = plane_ref[f, c, rows, :] + tiles[c]
            out_ref[f, rows, at] = fine_ref[f, rows, at] - DT_DX * change
        return carry

    lax.fori_loop(0, NF * blocks, turn, 0)


def register_kernel(got_ref, hot_ref, out_ref, z_ref):
    boxes = out_ref.shape[2]
    turned = got_ref[...].T
    parts = jnp.concatenate(split3(turned), axis=0)
    product = jnp.dot(parts, hot_ref[...], preferred_element_type=F32)
    z_ref[...] = product[0:LANES] + product[LANES : 2 * LANES] + product[2 * LANES :]
    for f in range(NF):
        for cx in range(CF):
            at = cx * TERM_ROWS + f * CF
            for s in range(SIDES):
                out_ref[f, pl.ds(s * CF * CF + cx, CF, stride=CF), :] = z_ref[
                    at : at + CF, s * boxes : (s + 1) * boxes
                ]


VM = pl.BlockSpec(memory_space=pltpu.VMEM)
SM = pl.BlockSpec(memory_space=pltpu.SMEM)


def call(body, name, ins, outs, scratch=(), cost=0, limit=24):
    return pl.pallas_call(
        body,
        name=name,
        in_specs=list(ins),
        out_specs=[VM] * len(outs) if len(outs) > 1 else VM,
        out_shape=outs if len(outs) > 1 else outs[0],
        scratch_shapes=list(scratch),
        compiler_params=pltpu.CompilerParams(vmem_limit_bytes=limit << 20),
        cost_estimate=pl.CostEstimate(flops=cost, bytes_accessed=cost, transcendentals=0),
    )


def shaped(*shape, dtype=F32):
    return jax.ShapeDtypeStruct(shape, dtype)


def local(members, groups, fine_state, coarse_boxes, piece_owner, piece_box):
    y_cells = fine_state.shape[1]
    x_cells = fine_state.shape[2] // PS
    boxes = coarse_boxes.shape[0]
    pieces = piece_box.shape[0]
    capacity = max(4, 2 * pieces // members)
    slots = members * capacity
    chunks = x_cells * PS // LANES
    patch_y = y_cells // PS
    assert chunks == PS and boxes == LANES and slots <= LANES and PS == QS
    assert y_cells == 4 * ROWS and pieces == SIDES * patch_y * (x_cells // PS)
    edge_rows = 2 * chunks
    rows_all = NF * QUANT * CF
    wide = SIDES * patch_y * LANES
    count = pltpu.SMEM((members,), I32)

    msg, low_edge, high_edge = call(
        functools.partial(prep_kernel, members, capacity, boxes),
        "prep",
        (SM, SM, VM),
        [
            shaped(members, (NF + 1) * ROWS, LANES),
            shaped(NF, edge_rows, LANES),
            shaped(NF, edge_rows, LANES),
        ],
        [count],
        cost=1 << 18,
    )(piece_owner, piece_box, fine_state)
    got = lax.all_to_all(msg, "dev", split_axis=0, concat_axis=0, tiled=True)
    up = [(g, (g + 1) % groups) for g in range(groups)]
    down = [(b, a) for a, b in up]
    y_low = lax.ppermute(high_edge, "group", up)
    y_high = lax.ppermute(low_edge, "group", down)

    wn, wz, zc, table, hot_fine = call(
        functools.partial(build_kernel, members, capacity),
        "build",
        (SM, VM, VM),
        [
            shaped(NF, chunks, y_cells, LANES),
            shaped(NF, PS, y_cells, LANES),
            shaped(NF, PS - 2, y_cells, LANES),
            shaped(3, TABLE_PAD, SIDES * boxes, dtype=BF16),
            shaped(CF * slots, wide, dtype=BF16),
        ],
        [
            count,
            pltpu.VMEM((NF, CB * CB * CB, boxes), F32),
        ],
        cost=1 << 23,
    )(piece_owner, fine_state, coarse_boxes)

    payload, hot_box = call(
        serve_kernel,
        "serve",
        (VM, VM),
        [shaped(slots, TABLE_PAD), shaped(slots, SIDES * boxes, dtype=BF16)],
        cost=1 << 18,
    )(got, table)
    back = lax.all_to_all(payload, "dev", split_axis=0, concat_axis=0, tiled=True)

    plane = call(
        functools.partial(plane_kernel, members),
        "plane",
        (VM, VM, VM, VM),
        [shaped(NF, chunks, y_cells, LANES)],
        cost=1 << 24,
    )(got, y_low, y_high, wn)

    terms, edge = call(
        functools.partial(face_kernel, slots),
        "face",
        (VM, VM, VM, VM),
        [shaped(slots, LANES), shaped(NF, 4, y_cells, LANES)],
        [
            pltpu.VMEM((TABLE_PAD, slots), F32),
            pltpu.VMEM((rows_all, CF * slots), F32),
            pltpu.VMEM((rows_all, wide), F32),
            pltpu.VMEM((SIDES, NF, y_cells, LANES), F32),
            pltpu.VMEM((TERM_ROWS, wide), F32),
        ],
        cost=1 << 20,
    )(back, hot_fine, wz, zc)
    incoming = lax.all_to_all(terms, "dev", split_axis=0, concat_axis=0, tiled=True)

    fine_next = call(
        final_kernel,
        "final",
        (VM, VM, VM, VM),
        [shaped(*fine_state.shape)],
        cost=1 << 23,
    )(fine_state, plane, zc, edge)
    flux_register = call(
        register_kernel,
        "register",
        (VM, VM),
        [shaped(NF, SIDES * CF * CF, boxes)],
        [pltpu.VMEM((LANES, SIDES * boxes), F32)],
        cost=1 << 18,
    )(incoming, hot_box)
    return (fine_next, flux_register)


def solution(mesh):
    in_specs = (
        P(None, "group", "dev"),
        P(("group", "dev"), None, None),
        P(("group", "dev"), None),
        P(("group", "dev")),
    )
    out_specs = (P(None, "group", "dev"), P(None, None, ("group", "dev")))
    body = functools.partial(local, mesh.shape["dev"], mesh.shape["group"])
    return jax.shard_map(body, mesh=mesh, in_specs=in_specs, out_specs=out_specs, check_vma=False)
```

time: 312 us -> 57.3 us (0.18); the launches traced: 306 us -> 56.7 us
  local copies, waits for them, and re-layouts: 199 us -> 10.3 us
  other arithmetic: 79.2 us -> 0 us
  Pallas kernels: 0 us -> 27.7 us
  starting transfers between devices: 23.6 us -> 16.5 us
    unnamed x206 -> x22, local copies, waits for them, and re-layouts: 46.4 us -> 10.3 us
    another operation x38 -> x0, local copies, waits for them, and re-layouts: 34.6 us -> none  [the longest x14 15.7 us: state_terms(): jnp.stack(flux_list)]
    slice x26 -> x0, local copies, waits for them, and re-layouts: 32.4 us -> none  [the longest x12 12.8 us: part_of(): return lax.slice_in_dim(array, start, stop, axis=dim_index)]
    pallas_call x0 -> x7, Pallas kernels: none -> 27.7 us  [the longest x1 8.94 us: local(): call(functools.partial(build_kernel, members, capacity), 'build', (SM, VM...]
    mul x25 -> x0, local copies, waits for them, and re-layouts: 26.2 us -> none  [the longest x4 5.62 us: state_terms(): density * primitive[2]]
    reshape x8 -> x0, local copies, waits for them, and re-layouts: 25.1 us -> none  [the longest x4 7.64 us: assemble(): chosen.transpose(4, 0, 3, 6, 5, 1, 2, 7)]
    unnamed x53 -> x0, other arithmetic: 23.2 us -> none
    sub x6 -> x0, other arithmetic: 13.2 us -> none  [the longest x2 9.46 us: face_fluxes(): primitive - 0.5 * slopes]
  transfers between devices with their start and end apart: 7 -> 5, of which waited for: 0 -> 1; matrix products, arithmetic and copies ran while one was open for 50% -> 4% of each run, Pallas kernels for 0% -> 44%
where the time goes in v1:
time: 57.3 us; the launch traced here: 56.7 us
  Pallas kernels  27.7 us (48%)
  starting transfers between devices  16.5 us (29%)
  local copies, waits for them, and re-layouts  10.3 us (18%)
  waiting for transfers between devices  1.38 us (2%)
  between operations  0.73 us (1%)
    unnamed x22, local copies, waits for them, and re-layouts  10.3 us
    pallas_call x1, Pallas kernels, local(): call(functools.partial(build_kernel, members, capacity), 'build', (SM, VM...  8.94 us
    pallas_call x1, Pallas kernels, local(): call(final_kernel, 'final', (VM, VM, VM, VM), [shaped(*fine_state.shape)]...  7.64 us
    pallas_call x1, Pallas kernels, local(): call(functools.partial(plane_kernel, members), 'plane', (VM, VM, VM, VM),...  6.54 us
    all_to_all x1, starting transfers between devices, local(): got = lax.all_to_all(msg, 'dev', split_axis=0, concat_axis=0, tiled=True)  5.2 us
    all_to_all x1, starting transfers between devices, local(): lax.all_to_all(payload, 'dev', split_axis=0, concat_axis=0, tiled=True)  4.19 us
    all_to_all x1, starting transfers between devices, local(): lax.all_to_all(terms, 'dev', split_axis=0, concat_axis=0, tiled=True)  3.32 us
    ppermute x1, starting transfers between devices, local(): y_high = lax.ppermute(low_edge, 'group', down)  2.25 us
  transfers between devices with their start and end apart: 5, of which 1 were waited for; matrix products, arithmetic and copies ran while one was open for 4% of the time, Pallas kernels for 44%

profile of v1, /device:TPU:0, one launch (start us, length us, event | category | flops | bytes accessed | tf_op | source)
XLA Modules:
  0.0 56.7 jit_solution(17575211910502060041)
XLA Ops:
  0.6 0.7 %copy.6.owner_ref = s32[32,1]{1,0:T(8,128)S(1)} copy(s32[32,1]{0,1:T(1,128)} %param.6) | data formatting | bytes 256 | tf_op args[2]
  1.4 1.3 %copy-done = f32[5,32,2048]{2,1,0:T(8,128)S(1)} copy-done((f32[5,32,2048]{2,1,0:T(8,128)S(1)}, f32[5,32,2048]{2,1,0:T(8,128)}, u32[]{:S(2)}) %copy-start) | copy-done | bytes 1310744
  2.7 0.7 %copy-done.7 = s32[32]{0:T(128)S(1)} copy-done((s32[32]{0:T(128)S(1)}, s32[32]{0:T(128)}, u32[]{:S(2)}) %copy-start.7) | copy-done | bytes 152
  3.3 1.7 %prep.1 = (f32[8,48,128]{2,1,0:T(8,128)}, f32[5,32,128]{2,1,0:T(8,128)S(1)}, f32[5,32,128]{2,1,0:T(8,128)S(1)}) custom-call(s32[32,1]{1,0:T(8,128)S(1)} %copy.6.owner_ref, s32[32]{0:T(128)S(1)} %copy-done.7, f32[5,32,2048]{2,1,0:T(8,128)S(1)} %copy-done), custom_call_target="tpu_custom_call" | custom-call | flops 262144 | bytes 262144 | tf_op jit(solution)/shard_map/prep/pallas_call | solution.py:586
  5.0 5.2 %all-to-all-start = ((f32[8,48,128]{2,1,0:T(8,128)}), f32[8,48,128]{2,1,0:T(8,128)S(1)}, u32[]{:S(2)}, u32[]{:S(2)}) async-start(f32[8,48,128]{2,1,0:T(8,128)} %get-tuple-element.14), calls=%async_computation | async-start | bytes 393216 | tf_op jit(solution)/shard_map/all_to_all | solution.py:598
  10.2 0.0 copy-done.8
  10.2 0.0 copy-done.9
  10.3 0.0 copy-start.1
  10.3 2.2 %copy.8.coarse_ref = f32[128,5,512]{2,1,0:T(8,128)S(1)} copy(f32[128,5,512]{2,0,1:T(8,128)} %param.5) | data formatting | bytes 2621440 | tf_op args[1]
  12.5 0.0 copy-done.1
  12.5 8.9 %build.1 = (f32[5,16,32,128]{3,2,1,0:T(8,128)S(1)}, f32[5,16,32,128]{3,2,1,0:T(8,128)S(1)}, f32[5,14,32,128]{3,2,1,0:T(8,128)S(1)}, bf16[3,384,256]{2,1,0:T(8,128)(2,1)S(1)}, bf16[256,512]{1,0:T(8,128)(2,1)S(1)}) custom-call(s32[32,1]{1,0:T(8,128)S(1)} %copy.6.owner_ref, f32[5,32,2048]{2,1,0:T(8,128)S(1)} %copy-done.1, f32[128,5,512]{2,1,0:T(8,128)S(1)} %copy.8.coarse_ref), custom_call_target="tpu_custom_call" | custom-call | flops 8388608 | bytes 8388608 | tf_op jit(solution)/shard_map/build/pallas_call | solution.py:604
  21.5 0.0 copy-start.2
  21.5 1.0 %copy-done.2 = f32[5,16,32,128]{3,2,1,0:T(8,128)} copy-done((f32[5,16,32,128]{3,2,1,0:T(8,128)}, f32[5,16,32,128]{3,2,1,0:T(8,128)S(1)}, u32[]{:S(2)}) %copy-start.2) | copy-done | bytes 1310744
  22.5 1.1 %copy-done.4 = f32[5,16,32,128]{3,2,1,0:T(8,128)} copy-done((f32[5,16,32,128]{3,2,1,0:T(8,128)}, f32[5,16,32,128]{3,2,1,0:T(8,128)S(1)}, u32[]{:S(2)}) %copy-start.4) | copy-done | bytes 1310744
  23.6 0.0 all-to-all-done.msg_ref
  23.6 0.3 serve.1
  23.9 0.6 %copy-done.6 = f32[64,384]{1,0:T(8,128)} copy-done((f32[64,384]{1,0:T(8,128)}, f32[64,384]{1,0:T(8,128)S(1)}, u32[]{:S(2)}) %copy-start.6) | copy-done | bytes 98328
  24.6 4.2 %all-to-all-start.1 = ((f32[8,8,384]{2,1,0:T(8,128)}), f32[8,8,384]{2,1,0:T(8,128)S(1)}, u32[]{:S(2)}, u32[]{:S(2)}) async-start(f32[8,8,384]{2,1,0:T(8,128)} %bitcast.6), calls=%async_computation.1 | async-start | bytes 196608 | tf_op jit(solution)/shard_map/all_to_all | solution.py:629
  28.8 1.6 %collective-permute-start = (f32[5,32,128]{2,1,0:T(8,128)}, f32[5,32,128]{2,1,0:T(8,128)S(1)}, u32[]{:S(2)}, u32[]{:S(2)}) collective-permute-start(f32[5,32,128]{2,1,0:T(8,128)} %copy-done.9), channel_id=1, source_target_pairs={{0,8},{8,16},{16,24},{24,0},{1,9},{9,17},{17,25},{25,1},{2,10},{10... | collective-permute-start | bytes 245768 | tf_op jit(solution)/shard_map/ppermute | solution.py:601
  30.3 2.2 %collective-permute-start.1 = (f32[5,32,128]{2,1,0:T(8,128)}, f32[5,32,128]{2,1,0:T(8,128)S(1)}, u32[]{:S(2)}, u32[]{:S(2)}) collective-permute-start(f32[5,32,128]{2,1,0:T(8,128)} %copy-done.8), channel_id=1, source_target_pairs={{8,0},{16,8},{24,16},{0,24},{9,1},{17,9},{25,17},{1,25},{10,2},{18... | collective-permute-start | bytes 245768 | tf_op jit(solution)/shard_map/ppermute | solution.py:602
  32.6 1.4 %all-to-all-done.1 = f32[8,8,384]{2,1,0:T(8,128)S(1)} async-done(((f32[8,8,384]{2,1,0:T(8,128)}), f32[8,8,384]{2,1,0:T(8,128)S(1)}, u32[]{:S(2)}, u32[]{:S(2)}) %all-to-all-start.1) | async-done | bytes 98336 | tf_op jit(solution)/shard_map/all_to_all | solution.py:629
  34.0 1.3 %copy-done.5 = f32[5,16,32,128]{3,2,1,0:T(8,128)S(1)} copy-done((f32[5,16,32,128]{3,2,1,0:T(8,128)S(1)}, f32[5,16,32,128]{3,2,1,0:T(8,128)}, u32[]{:S(2)}) %copy-start.5) | copy-done | bytes 1310744
  35.3 1.7 %face.1 = (f32[64,128]{1,0:T(8,128)}, f32[5,4,32,128]{3,2,1,0:T(8,128)S(1)}) custom-call(f32[64,384]{1,0:T(8,128)S(1)} %bitcast.4, bf16[256,512]{1,0:T(8,128)(2,1)S(1)} %get-tuple-element.21.he_ref, f32[5,16,32,128]{3,2,1,0:T(8,128)S(1)} %copy-done.5, f32[5,14,32,128]{3,2,1,0:T(8,128)S(1)} %get-tuple-element.18.zc_ref), custom_call_target="tpu_custom_call" | custom-call | flops 1048576 | bytes 1048576 | tf_op jit(solution)/shard_map/face/pallas_call | solution.py:639
  37.0 3.3 %all-to-all-start.2 = ((f32[8,8,128]{2,1,0:T(8,128)}), f32[8,8,128]{2,1,0:T(8,128)S(1)}, u32[]{:S(2)}, u32[]{:S(2)}) async-start(f32[8,8,128]{2,1,0:T(8,128)} %bitcast.2), calls=%async_computation.2 | async-start | bytes 65536 | tf_op jit(solution)/shard_map/all_to_all | solution.py:653
  40.3 0.0 collective-permute-done.lo_ref
  40.3 0.0 collective-permute-done.1.hi_ref
  40.3 0.0 copy-start.3
  40.3 1.3 %copy-done.3 = f32[5,16,32,128]{3,2,1,0:T(8,128)S(1)} copy-done((f32[5,16,32,128]{3,2,1,0:T(8,128)S(1)}, f32[5,16,32,128]{3,2,1,0:T(8,128)}, u32[]{:S(2)}) %copy-start.3) | copy-done | bytes 1310744
  41.6 6.5 %plane.1.plane_ref = f32[5,16,32,128]{3,2,1,0:T(8,128)S(1)} custom-call(f32[8,48,128]{2,1,0:T(8,128)S(1)} %all-to-all-done.msg_ref, f32[5,32,128]{2,1,0:T(8,128)S(1)} %collective-permute-done.lo_ref, f32[5,32,128]{2,1,0:T(8,128)S(1)} %collective-permute-done.1.hi_ref, f32[5,16,32,128]{3,2,1,0:T(8,128)S(1)} %copy-done.3), custom_call_target="tpu_custom_call" | custom-call | flops 16777216 | bytes 16777216 | tf_op jit(solution)/shard_map/plane/pallas_call | solution.py:631
  48.2 7.6 %final.1 = f32[5,32,2048]{2,1,0:T(8,128)} custom-call(f32[5,32,2048]{2,1,0:T(8,128)S(1)} %copy-done.1, f32[5,16,32,128]{3,2,1,0:T(8,128)S(1)} %plane.1.plane_ref, f32[5,14,32,128]{3,2,1,0:T(8,128)S(1)} %get-tuple-element.18.zc_ref, f32[5,4,32,128]{3,2,1,0:T(8,128)S(1)} %get-tuple-element.23.edge_ref), custom_call_target="tpu_custom_call" | custom-call | flops 8388608 | bytes 8388608 | tf_op jit(solution)/shard_map/final/pallas_call | solution.py:655
  55.8 0.0 all-to-all-done.2
  55.8 0.9 %register.1 = f32[5,32,128]{2,1,0:T(8,128)} custom-call(f32[64,128]{1,0:T(8,128)S(1)} %bitcast.5, bf16[64,256]{1,0:T(8,128)(2,1)S(1)} %get-tuple-element.25.hot_ref), custom_call_target="tpu_custom_call" | custom-call | flops 262144 | bytes 262144 | tf_op jit(solution)/shard_map/register/pallas_call | solution.py:662
  (7 shorter events, 0.0 us)
Async XLA Ops:
  1.4 1.3 %copy-start = (f32[5,32,2048]{2,1,0:T(8,128)S(1)}, f32[5,32,2048]{2,1,0:T(8,128)}, u32[]{:S(2)}) copy-start(f32[5,32,2048]{2,1,0:T(8,128)} %fine_ref.5) | copy-start | bytes 3932164
  2.7 0.7 %copy-start.7 = (s32[32]{0:T(128)S(1)}, s32[32]{0:T(128)}, u32[]{:S(2)}) copy-start(s32[32]{0:T(128)} %box_ref.1) | copy-start | bytes 388
  5.0 5.2 %copy-start.8 = (f32[5,32,128]{2,1,0:T(8,128)}, f32[5,32,128]{2,1,0:T(8,128)S(1)}, u32[]{:S(2)}) copy-start(f32[5,32,128]{2,1,0:T(8,128)S(1)} %get-tuple-element.16) | copy-start | bytes 245764
  5.0 5.2 %copy-start.9 = (f32[5,32,128]{2,1,0:T(8,128)}, f32[5,32,128]{2,1,0:T(8,128)S(1)}, u32[]{:S(2)}) copy-start(f32[5,32,128]{2,1,0:T(8,128)S(1)} %get-tuple-element.15) | copy-start | bytes 245764
  5.0 18.6 %all-to-all-start = ((f32[8,48,128]{2,1,0:T(8,128)}), f32[8,48,128]{2,1,0:T(8,128)S(1)}, u32[]{:S(2)}, u32[]{:S(2)}) async-start(f32[8,48,128]{2,1,0:T(8,128)} %get-tuple-element.14), calls=%async_computation | async-start | bytes 393216 | tf_op jit(solution)/shard_map/all_to_all | solution.py:598
  10.3 2.2 %copy-start.1 = (f32[5,32,2048]{2,1,0:T(8,128)S(1)}, f32[5,32,2048]{2,1,0:T(8,128)}, u32[]{:S(2)}) copy-start(f32[5,32,2048]{2,1,0:T(8,128)} %fine_ref.5) | copy-start | bytes 3932164
  21.5 1.1 %copy-start.2 = (f32[5,16,32,128]{3,2,1,0:T(8,128)}, f32[5,16,32,128]{3,2,1,0:T(8,128)S(1)}, u32[]{:S(2)}) copy-start(f32[5,16,32,128]{3,2,1,0:T(8,128)S(1)} %get-tuple-element.17.wn_ref) | copy-start | bytes 3932164
  22.5 1.1 %copy-start.4 = (f32[5,16,32,128]{3,2,1,0:T(8,128)}, f32[5,16,32,128]{3,2,1,0:T(8,128)S(1)}, u32[]{:S(2)}) copy-start(f32[5,16,32,128]{3,2,1,0:T(8,128)S(1)} %get-tuple-element.22.wz_ref) | copy-start | bytes 3932164
  23.9 0.6 %copy-start.6 = (f32[64,384]{1,0:T(8,128)}, f32[64,384]{1,0:T(8,128)S(1)}, u32[]{:S(2)}) copy-start(f32[64,384]{1,0:T(8,128)S(1)} %get-tuple-element.20) | copy-start | bytes 294916
  24.6 9.4 %all-to-all-start.1 = ((f32[8,8,384]{2,1,0:T(8,128)}), f32[8,8,384]{2,1,0:T(8,128)S(1)}, u32[]{:S(2)}, u32[]{:S(2)}) async-start(f32[8,8,384]{2,1,0:T(8,128)} %bitcast.6), calls=%async_computation.1 | async-start | bytes 196608 | tf_op jit(solution)/shard_map/all_to_all | solution.py:629
  28.8 11.5 %collective-permute-start = (f32[5,32,128]{2,1,0:T(8,128)}, f32[5,32,128]{2,1,0:T(8,128)S(1)}, u32[]{:S(2)}, u32[]{:S(2)}) collective-permute-start(f32[5,32,128]{2,1,0:T(8,128)} %copy-done.9), channel_id=1, source_target_pairs={{0,8},{8,16},{16,24},{24,0},{1,9},{9,17},{17,25},{25,1},{2,10},{10... | collective-permute-start | bytes 245768 | tf_op jit(solution)/shard_map/ppermute | solution.py:601
  30.3 10.0 %collective-permute-start.1 = (f32[5,32,128]{2,1,0:T(8,128)}, f32[5,32,128]{2,1,0:T(8,128)S(1)}, u32[]{:S(2)}, u32[]{:S(2)}) collective-permute-start(f32[5,32,128]{2,1,0:T(8,128)} %copy-done.8), channel_id=1, source_target_pairs={{8,0},{16,8},{24,16},{0,24},{9,1},{17,9},{25,17},{1,25},{10,2},{18... | collective-permute-start | bytes 245768 | tf_op jit(solution)/shard_map/ppermute | solution.py:602
  34.0 1.3 %copy-start.5 = (f32[5,16,32,128]{3,2,1,0:T(8,128)S(1)}, f32[5,16,32,128]{3,2,1,0:T(8,128)}, u32[]{:S(2)}) copy-start(f32[5,16,32,128]{3,2,1,0:T(8,128)} %copy-done.4) | copy-start | bytes 3932164
  37.0 18.9 %all-to-all-start.2 = ((f32[8,8,128]{2,1,0:T(8,128)}), f32[8,8,128]{2,1,0:T(8,128)S(1)}, u32[]{:S(2)}, u32[]{:S(2)}) async-start(f32[8,8,128]{2,1,0:T(8,128)} %bitcast.2), calls=%async_computation.2 | async-start | bytes 65536 | tf_op jit(solution)/shard_map/all_to_all | solution.py:653
  40.3 1.3 %copy-start.3 = (f32[5,16,32,128]{3,2,1,0:T(8,128)S(1)}, f32[5,16,32,128]{3,2,1,0:T(8,128)}, u32[]{:S(2)}) copy-start(f32[5,16,32,128]{3,2,1,0:T(8,128)} %copy-done.2) | copy-start | bytes 3932164

commit v2 on v1

--- a/solution.py
+++ b/solution.py
@@ -99,20 +99,38 @@
         count_ref[m] = 0
     slots = []
     for p in range(pieces):
-        owner = owner_ref[p, 0]
+        owner = owner_ref[p]
         rank = count_ref[owner]
         count_ref[owner] = rank + 1
         slots.append(owner * capacity + rank)
     return slots
 
 
-def prep_kernel(members, capacity, boxes, owner_ref, box_ref, fine_ref, msg_ref, lo_ref, hi_ref, count_ref):
+def prep_kernel(
+    members, capacity, boxes, owner_hbm, box_hbm, fine_hbm, msg_hbm, lo_hbm, hi_hbm, code_ref,
+    owner_ref, box_ref, count_ref, low_ref, high_ref, left_ref, right_ref,
+    msg_ref, lo_ref, hi_ref, sem_ref, out_sem,
+):
     me = lax.axis_index("dev")
-    pieces = box_ref.shape[0]
-    chunks = fine_ref.shape[2] // LANES
-    blocks = fine_ref.shape[1] // ROWS
+    pieces = box_hbm.shape[0]
+    y_cells = fine_hbm.shape[1]
+    chunks = fine_hbm.shape[2] // LANES
+    blocks = y_cells // ROWS
+    ends = [
+        (owner_hbm, owner_ref),
+        (box_hbm, box_ref),
+        (fine_hbm.at[:, :, 0:LANES], left_ref),
+        (fine_hbm.at[:, :, (chunks - 1) * LANES : chunks * LANES], right_ref),
+        (fine_hbm.at[:, 0:ROWS, :], low_ref),
+        (fine_hbm.at[:, y_cells - ROWS : y_cells, :], high_ref),
+    ]
+    copies = [pltpu.make_async_copy(a, b, sem_ref.at[i]) for i, (a, b) in enumerate(ends)]
+    for copy in copies:
+        copy.start()
     lane = iota((ROWS, LANES), 1)
     sub = iota((ROWS, LANES), 0)
+    copies[0].wait()
+    copies[1].wait()
     slots = count_slots(owner_ref, count_ref, members, capacity, pieces)
     values = jnp.zeros((ROWS, LANES), I32)
     for p in range(pieces):
@@ -123,98 +141,25 @@
         shift = lax.rem((me - m) * capacity + LANES * members, LANES)
         msg_ref[m, NF * ROWS :, :] = jnp.where(mine, pltpu.roll(values, shift, 1), 0.0)
     width = 2 * PS
+    copies[2].wait()
+    copies[3].wait()
     for f in range(NF):
-        left = fine_ref[f, 0:ROWS, 0:LANES]
-        right = pltpu.roll(fine_ref[f, 0:ROWS, (chunks - 1) * LANES :], width, 1)
+        left = left_ref[f, 0:ROWS, :]
+        right = pltpu.roll(right_ref[f, 0:ROWS, :], width, 1)
         for g in range(1, blocks):
             rows = slice(g * ROWS, (g + 1) * ROWS)
             here = lane // width == g
-            left = jnp.where(here, pltpu.roll(fine_ref[f, rows, 0:LANES], width * g, 1), left)
-            edge = fine_ref[f, rows, (chunks - 1) * LANES :]
+            left = jnp.where(here, pltpu.roll(left_ref[f, rows, :], width * g, 1), left)
+            edge = right_ref[f, rows, :]
             shift = (width * (g + 1)) % LANES
             right = jnp.where(here, pltpu.roll(edge, shift, 1) if shift else edge, right)
         for m in range(members):
             below = jnp.full((ROWS, LANES), m, I32) < me
             msg_ref[m, f * ROWS : (f + 1) * ROWS, :] = jnp.where(below, left, right)
-    for f in range(NF):
-        for j in range(chunks // 4):
-            low = high = None
-            for k in range(4):
-                c = slice((4 * j + k) * LANES, (4 * j + k + 1) * LANES)
-                first = fine_ref[f, 0:ROWS, c]
-                last = fine_ref[f, (blocks - 1) * ROWS :, c]
-                first = pltpu.roll(first, 2 * k, 0) if k else first
-                last = pltpu.roll(last, 2 * k + 2, 0) if k < 3 else last
-                low = first if k == 0 else jnp.where(sub // 2 == k, first, low)
-                high = last if k == 0 else jnp.where(sub // 2 == k, last, high)
-            lo_ref[f, j * ROWS : (j + 1) * ROWS, :] = low
-            hi_ref[f, j * ROWS : (j + 1) * ROWS, :] = high
-
-
-def build_kernel(
-    members, capacity, owner_ref, fine_ref, coarse_ref,
-    wn_ref, wz_ref, zc_ref, tab_ref, he_ref,
-    count_ref, ct_ref,
-):
-    lane = iota((ROWS, LANES), 1)
-    sub = iota((ROWS, LANES), 0)
-    chunks = fine_ref.shape[2] // LANES
-    blocks = fine_ref.shape[1] // ROWS
-    patch_y = fine_ref.shape[1] // PS
+    outs = [pltpu.make_async_copy(msg_ref, msg_hbm, out_sem.at[0])]
+    outs[0].start()
+    patch_y = y_cells // PS
     patch_x = chunks * LANES // PS // PS
-    pieces = owner_ref.shape[0]
-    slot_count = members * capacity
-
-    def primitive_block(block, carry):
-        rows = pl.ds(pl.multiple_of(block * ROWS, ROWS), ROWS)
-        for c in range(chunks):
-            prim = to_primitive(
-                [fine_ref[f, rows, c * LANES : (c + 1) * LANES] for f in range(NF)]
-            )
-            for f in range(NF):
-                wn_ref[f, c, rows, :] = prim[f]
-        return carry
-
-    lax.fori_loop(0, blocks, primitive_block, 0)
-
-    def turn(step, carry):
-        f = step // blocks
-        rows = pl.ds(pl.multiple_of((step % blocks) * ROWS, ROWS), ROWS)
-        tiles = swap_groups([wn_ref[f, c, rows, :] for c in range(chunks)], lane)
-        for z in range(PS):
-            wz_ref[f, z, rows, :] = tiles[z]
-        return carry
-
-    lax.fori_loop(0, NF * blocks, turn, 0)
-
-    def sweep(block, carry):
-        rows = pl.ds(pl.multiple_of(block * ROWS, ROWS), ROWS)
-
-        def load(z):
-            return [wz_ref[f, z, rows, :] for f in range(NF)]
-
-        w_here = load(1)
-        w_before = load(0)
-        diff = [w_here[f] - w_before[f] for f in range(NF)]
-        low = flux = None
-        for z in range(1, PS - 1):
-            w_next = load(z + 1)
-            diff_next = [w_next[f] - w_here[f] for f in range(NF)]
-            half = [0.5 * minmod(diff[f], diff_next[f]) for f in range(NF)]
-            if z >= 2:
-                new = hll(low, [w_here[f] - half[f] for f in range(NF)], 2)
-                for f in range(NF):
-                    zc_ref[f, z - 2, rows, :] = new[f] if z == 2 else new[f] - flux[f]
-                flux = new
-            low = [w_here[f] + half[f] for f in range(NF)]
-            w_here, diff = w_next, diff_next
-        for f in range(NF):
-            zc_ref[f, PS - 3, rows, :] = -flux[f]
-        return carry
-
-    lax.fori_loop(0, blocks, sweep, 0)
-
-    slots = count_slots(owner_ref, count_ref, members, capacity, pieces)
     x_cell = (lane % PS) * (LANES // PS) + lane // PS
     for s in range(SIDES):
         for ky in range(patch_y):
@@ -222,17 +167,64 @@
             for kx in range(patch_x):
                 slot = slots[(ky * patch_x + kx) * SIDES + s]
                 code = jnp.where(x_cell // PS == kx, slot, code)
-            code = code + (x_cell // RATIO) % CF * slot_count
-            at = (s * patch_y + ky) * LANES
-            hot = iota((CF * slot_count, LANES), 0) == code[0:1, :]
-            he_ref[:, at : at + LANES] = jnp.where(hot, 1.0, 0.0).astype(BF16)
-
-    boxes = coarse_ref.shape[0]
+            code_ref[s * patch_y + ky] = code + (x_cell // RATIO) % CF * (members * capacity)
+    copies[4].wait()
+    copies[5].wait()
     for f in range(NF):
+        for j in range(chunks // 4):
+            low = high = None
+            for k in range(4):
+                c = slice((4 * j + k) * LANES, (4 * j + k + 1) * LANES)
+                first = low_ref[f, :, c]
+                last = high_ref[f, :, c]
+                first = pltpu.roll(first, 2 * k, 0) if k else first
+                last = pltpu.roll(last, 2 * k + 2, 0) if k < 3 else last
+                low = first if k == 0 else jnp.where(sub // 2 == k, first, low)
+                high = last if k == 0 else jnp.where(sub // 2 == k, last, high)
+            lo_ref[f, j * ROWS : (j + 1) * ROWS, :] = low
+            hi_ref[f, j * ROWS : (j + 1) * ROWS, :] = high
+    outs.append(pltpu.make_async_copy(lo_ref, lo_hbm, out_sem.at[1]))
+    outs.append(pltpu.make_async_copy(hi_ref, hi_hbm, out_sem.at[2]))
+    outs[1].start()
+    outs[2].start()
+    for copy in outs:
+        copy.wait()
+
+
+def build_kernel(fine_ref, coarse_hbm, wz_ref, tab_ref, wn_ref, cs_ref, ct_ref, coarse_sem):
+    chunks = fine_ref.shape[2] // LANES
+    blocks = fine_ref.shape[1] // ROWS
+    coarse_copies = [
+        pltpu.make_async_copy(coarse_hbm.at[f], cs_ref.at[f], coarse_sem.at[f]) for f in range(NF)
+    ]
+    for copy in coarse_copies:
+        copy.start()
+    lane = iota((ROWS, LANES), 1)
+    sub = iota((ROWS, LANES), 0)
+
+    def turn(block, carry):
+        rows = pl.ds(pl.multiple_of(block * ROWS, ROWS), ROWS)
+        for c in range(chunks):
+            prim = to_primitive(
+                [fine_ref[f, rows, c * LANES : (c + 1) * LANES] for f in range(NF)]
+            )
+            for f in range(NF):
+                wn_ref[f, c] = prim[f]
+        for f in range(NF):
+            tiles = swap_groups([wn_ref[f, c] for c in range(chunks)], lane)
+            for z in range(PS):
+                wz_ref[f, z, rows, :] = tiles[z]
+        return carry
+
+    lax.fori_loop(0, blocks, turn, 0)
+
+    boxes = coarse_hbm.shape[1]
+    for f in range(NF):
+        coarse_copies[f].wait()
         for j in range(CB * CB * CB // LANES):
             at = slice(j * LANES, (j + 1) * LANES)
-            ct_ref[f, at, :] = coarse_ref[:, f, at].T
-    tab_ref[:, TABLE_ROWS:, :] = jnp.zeros((3, TABLE_PAD - TABLE_ROWS, SIDES * boxes), BF16)
+            ct_ref[f, at, :] = cs_ref[f, :, at].T
+    tab_ref[TABLE_ROWS:, :] = jnp.zeros((TABLE_PAD - TABLE_ROWS, SIDES * boxes), F32)
     for s in range(SIDES):
         middle = CB - 3 if s == 0 else 2
 
@@ -253,21 +245,18 @@
                 found[f, 3, cy] = minmod(c - pltpu.roll(c, 1, 0), pltpu.roll(c, ROWS - 1, 0) - c)
         for f in range(NF):
             for q in range(QUANT):
-                halves = [
-                    jnp.where(
-                        sub < CF,
-                        pltpu.roll(found[f, q, 2 * i], ROWS - 2, 0),
-                        pltpu.roll(found[f, q, 2 * i + 1], 2, 0),
+                at = (f * QUANT + q) * CF * CF
+                for i in range(2):
+                    tab_ref[at + i * ROWS : at + (i + 1) * ROWS, s * boxes : (s + 1) * boxes] = (
+                        jnp.where(
+                            sub < CF,
+                            pltpu.roll(found[f, q, 2 * i], ROWS - 2, 0),
+                            pltpu.roll(found[f, q, 2 * i + 1], 2, 0),
+                        )
                     )
-                    for i in range(2)
-                ]
-                tile = jnp.concatenate(halves, axis=0)
-                at = (f * QUANT + q) * CF * CF
-                for number, part in enumerate(split3(tile)):
-                    tab_ref[number, at : at + CF * CF, s * boxes : (s + 1) * boxes] = part
-
-
-def serve_kernel(msg_ref, tab_ref, out_ref, hot_ref):
+
+
+def serve_kernel(msg_ref, tab_ref, out_hbm, hot_ref, out_ref, sem_ref):
     members = msg_ref.shape[0]
     slot_count = out_ref.shape[0]
     row = msg_ref[0, NF * ROWS :, :]
@@ -280,21 +269,20 @@
     hot = jnp.where(iota(hot_ref.shape, 1) == target, 1.0, 0.0).astype(BF16)
     hot_ref[...] = hot
     total = None
-    for part in range(3):
+    for part in split3(tab_ref[...]):
         got = lax.dot_general(
-            hot, tab_ref[part], (((1,), (1,)), ((), ())), preferred_element_type=F32
+            hot, part, (((1,), (1,)), ((), ())), preferred_element_type=F32
         )
         total = got if total is None else total + got
     out_ref[...] = total
-
-
-def sweep_line(tiles, normal, back, forward, emit):
+    copy = pltpu.make_async_copy(out_ref, out_hbm, sem_ref.at[0])
+    copy.start()
+    copy.wait()
+
+
+def sweep_line(tiles, normal, back, forward, emit, finish=None):
     fields = range(NF)
     last = len(tiles) - 1
-
-    def join_back(before, here):
-        return [back(before[f], here[f]) for f in fields]
-
     moved = [[back(None, t[f]) for f in fields] for t in tiles]
     diff = [
         [t[f] - back(moved[max(i - 1, 0)][f], moved[i][f]) for f in fields]
@@ -308,6 +296,9 @@
             0.5 * minmod(diff[i][f], forward(diff_moved[i][f], diff_moved[min(i + 1, last)][f]))
             for f in fields
         ]
+        if i == last and finish is not None:
+            finish(low_moved, [t[f] - half[f] for f in fields], flux, flux_moved)
+            return
         low_next = [back(None, t[f] + half[f]) for f in fields]
         if i > 0:
             left = [back(low_moved[f], low_next[f]) for f in fields]
@@ -319,10 +310,12 @@
         low_moved = low_next
 
 
-def plane_kernel(members, msg_ref, lo_ref, hi_ref, wn_ref, out_ref):
+def plane_kernel(
+    members, msg_ref, lo_ref, hi_ref, fine_ref, after_ref, out_ref, wn_ref
+):
     me = lax.axis_index("dev")
-    chunks = wn_ref.shape[1]
-    blocks = wn_ref.shape[2] // ROWS
+    chunks = fine_ref.shape[2] // LANES
+    blocks = fine_ref.shape[1] // ROWS
     lane = iota((ROWS, LANES), 1)
     sub = iota((ROWS, LANES), 0)
     width = 2 * PS
@@ -350,7 +343,14 @@
         high = to_primitive(
             [pltpu.roll(msg_ref[right, f * ROWS : (f + 1) * ROWS, :], shift_high, 1) for f in range(NF)]
         )
-        tiles = [[wn_ref[f, c, rows, :] for f in range(NF)] for c in range(chunks)]
+        tiles = []
+        for c in range(chunks):
+            prim = to_primitive(
+                [fine_ref[f, rows, c * LANES : (c + 1) * LANES] for f in range(NF)]
+            )
+            for f in range(NF):
+                wn_ref[f, c, rows, :] = prim[f]
+            tiles.append(prim)
         for f in range(NF):
             w = tiles[0][f]
             same = jnp.where(
@@ -362,8 +362,9 @@
             high[f] = jnp.where(place == members - 1, same, high[f])
 
         def emit(c, change):
+            at = slice(c * LANES, (c + 1) * LANES)
             for f in range(NF):
-                out_ref[f, c, rows, :] = change[f]
+                out_ref[f, c, rows, :] = fine_ref[f, rows, at] - DT_DX * change[f]
 
         sweep_line([low] + tiles + [high], 0, x_back, x_forward, emit)
         return carry
@@ -381,13 +382,16 @@
         return jnp.where(sub >= ROWS - 1, after, here)
 
     def y_block(j, carry):
-        rows = pl.ds(pl.multiple_of(j * ROWS, ROWS), ROWS)
-        low = to_primitive([lo_ref[f, rows, :] for f in range(NF)])
-        high = to_primitive([hi_ref[f, rows, :] for f in range(NF)])
-        for k in range(4):
-            c = 4 * j + k
-            below = [pltpu.roll(t, (ROWS - 2 - 2 * k) % ROWS, 0) if k < 3 else t for t in low]
-            above = [pltpu.roll(t, ROWS - 2 * k, 0) if k else t for t in high]
+        ends = []
+        for k in range(ROWS):
+            at = pl.ds(pl.multiple_of((2 * j + k // 4) * ROWS, ROWS), ROWS)
+            if k % 4 == 0:
+                low = to_primitive([lo_ref[f, at, :] for f in range(NF)])
+                high = to_primitive([hi_ref[f, at, :] for f in range(NF)])
+            c = ROWS * j + k
+            turn_low, turn_high = (6 - 2 * (k % 4)) % ROWS, (ROWS - 2 * (k % 4)) % ROWS
+            below = [pltpu.roll(t, turn_low, 0) if turn_low else t for t in low]
+            above = [pltpu.roll(t, turn_high, 0) if turn_high else t for t in high]
             tiles = [
                 [wn_ref[f, c, b * ROWS : (b + 1) * ROWS, :] for f in range(NF)]
                 for b in range(blocks)
@@ -396,17 +400,37 @@
             def emit(b, change):
                 at = slice(b * ROWS, (b + 1) * ROWS)
                 for f in range(NF):
-                    out_ref[f, c, at, :] = out_ref[f, c, at, :] + change[f]
-
-            sweep_line([below] + tiles + [above], 1, y_back, y_forward, emit)
+                    out_ref[f, c, at, :] = out_ref[f, c, at, :] - DT_DX * change[f]
+
+            sweep_line(
+                [below] + tiles + [above], 1, y_back, y_forward, emit, lambda *end: ends.append(end)
+            )
+        packed = []
+        for which in range(2):
+            state = []
+            for f in range(NF):
+                tile = ends[0][which][f]
+                for k in range(1, ROWS):
+                    tile = jnp.where(sub == k, pltpu.roll(ends[k][which][f], k, 0), tile)
+                state.append(tile)
+            packed.append(state)
+        top = hll(packed[0], packed[1], 1)
+        at = slice((blocks - 1) * ROWS, blocks * ROWS)
+        for k in range(ROWS):
+            c = ROWS * j + k
+            flux, flux_moved = ends[k][2], ends[k][3]
+            for f in range(NF):
+                moved = pltpu.roll(top[f], ROWS - 1 - k, 0) if k < ROWS - 1 else top[f]
+                change = y_forward(flux_moved[f], moved) - flux[f]
+                out_ref[f, c, at, :] = out_ref[f, c, at, :] - DT_DX * change
         return carry
 
-    lax.fori_loop(0, chunks // 4, y_block, 0)
+    lax.fori_loop(0, chunks // ROWS, y_block, 0)
 
 
 def face_kernel(
-    slot_count, got_ref, he_ref, wz_ref, zc_ref, term_ref, edge_ref,
-    rt_ref, lf_ref, g_ref, fs_ref, v_ref,
+    slot_count, got_ref, code_ref, wz_ref, after_ref, term_hbm, edge_ref,
+    he_ref, rt_ref, lf_ref, g_ref, fs_ref, v_ref, term_ref, sem_ref,
 ):
     lane = iota((ROWS, LANES), 1)
     sub = iota((ROWS, LANES), 0)
@@ -414,6 +438,10 @@
     y_cells = wz_ref.shape[2]
     blocks = y_cells // ROWS
     patch_y = y_cells // PS
+    number = iota((CF * slot_count, LANES), 0)
+    for i in range(code_ref.shape[0]):
+        hot = jnp.where(number == code_ref[i, 0:1, :], 1.0, 0.0)
+        he_ref[:, i * LANES : (i + 1) * LANES] = hot.astype(BF16)
     rt_ref[...] = got_ref[...].T
     for cx in range(CF):
         lf_ref[:, cx * slot_count : (cx + 1) * slot_count] = rt_ref[
@@ -456,13 +484,11 @@
                         ((terms[0] + terms[1] * off_z) + terms[2] * off_y) + terms[3] * off_x
                     )
 
-            def load(z):
-                return [wz_ref[f, z, rows, :] for f in range(NF)]
-
-            if s == 0:
-                line = ghosts + [load(0), load(1), load(2)]
-            else:
-                line = [load(PS - 3), load(PS - 2), load(PS - 1)] + ghosts
+            inner = [
+                [wz_ref[f, z, rows, :] for f in range(NF)]
+                for z in (range(3) if s == 0 else range(PS - 3, PS))
+            ]
+            line = ghosts + inner if s == 0 else inner + ghosts
             diff = [[line[i + 1][f] - line[i][f] for f in range(NF)] for i in range(4)]
             half_slope = [
                 [0.5 * minmod(diff[i][f], diff[i + 1][f]) for f in range(NF)] for i in range(3)
@@ -478,10 +504,10 @@
             for f in range(NF):
                 if s == 0:
                     edge_ref[f, 0, rows, :] = flux[1][f] - flux[0][f]
-                    edge_ref[f, 1, rows, :] = zc_ref[f, 0, rows, :] - flux[1][f]
+                    edge_ref[f, 1, rows, :] = -flux[1][f]
                     fs_ref[0, f, rows, :] = flux[0][f]
                 else:
-                    edge_ref[f, 2, rows, :] = zc_ref[f, PS - 3, rows, :] + flux[0][f]
+                    edge_ref[f, 2, rows, :] = flux[0][f]
                     edge_ref[f, 3, rows, :] = flux[1][f] - flux[0][f]
                     fs_ref[1, f, rows, :] = flux[1][f]
 
@@ -508,27 +534,62 @@
         term_ref[:, cx * TERM_ROWS : (cx + 1) * TERM_ROWS] = turned[
             cx * slot_count : (cx + 1) * slot_count, :
         ]
-
-
-def final_kernel(fine_ref, plane_ref, zc_ref, edge_ref, out_ref):
+    copy = pltpu.make_async_copy(term_ref, term_hbm, sem_ref.at[0])
+    copy.start()
+    copy.wait()
+
+
+def final_kernel(
+    wz_ref, plane_ref, edge_ref, out_hbm, zc_ref, out_ref, out_sem
+):
     lane = iota((ROWS, LANES), 1)
     chunks = plane_ref.shape[1]
     blocks = plane_ref.shape[2] // ROWS
 
-    def turn(step, carry):
-        f = step // blocks
-        rows = pl.ds(pl.multiple_of((step % blocks) * ROWS, ROWS), ROWS)
-        tiles = [edge_ref[f, 0, rows, :], edge_ref[f, 1, rows, :]]
-        tiles += [zc_ref[f, z - 1, rows, :] for z in range(2, PS - 2)]
-        tiles += [edge_ref[f, 2, rows, :], edge_ref[f, 3, rows, :]]
-        tiles = swap_groups(tiles, lane)
-        for c in range(chunks):
-            at = slice(c * LANES, (c + 1) * LANES)
-            change = plane_ref[f, c, rows, :] + tiles[c]
-            out_ref[f, rows, at] = fine_ref[f, rows, at] - DT_DX * change
+    def out_copy(block):
+        rows = pl.ds(pl.multiple_of(block * ROWS, ROWS), ROWS)
+        return pltpu.make_async_copy(
+            out_ref.at[:, rows, :], out_hbm.at[:, rows, :], out_sem.at[block]
+        )
+
+    def step(block, carry):
+        rows = pl.ds(pl.multiple_of(block * ROWS, ROWS), ROWS)
+
+        def load(z):
+            return [wz_ref[f, z, rows, :] for f in range(NF)]
+
+        w_here = load(1)
+        w_before = load(0)
+        diff = [w_here[f] - w_before[f] for f in range(NF)]
+        low = flux = None
+        for z in range(1, PS - 1):
+            w_next = load(z + 1)
+            diff_next = [w_next[f] - w_here[f] for f in range(NF)]
+            half = [0.5 * minmod(diff[f], diff_next[f]) for f in range(NF)]
+            if z >= 2:
+                new = hll(low, [w_here[f] - half[f] for f in range(NF)], 2)
+                for f in range(NF):
+                    before = edge_ref[f, 1, rows, :] if z == 2 else -flux[f]
+                    zc_ref[f, z - 2] = new[f] + before
+                flux = new
+            low = [w_here[f] + half[f] for f in range(NF)]
+            w_here, diff = w_next, diff_next
+        for f in range(NF):
+            zc_ref[f, PS - 3] = edge_ref[f, 2, rows, :] - flux[f]
+        for f in range(NF):
+            tiles = [edge_ref[f, 0, rows, :]]
+            tiles += [zc_ref[f, z] for z in range(PS - 2)]
+            tiles += [edge_ref[f, 3, rows, :]]
+            tiles = swap_groups(tiles, lane)
+            for c in range(chunks):
+                at = slice(c * LANES, (c + 1) * LANES)
+                out_ref[f, rows, at] = plane_ref[f, c, rows, :] - DT_DX * tiles[c]
+        out_copy(block).start()
         return carry
 
-    lax.fori_loop(0, NF * blocks, turn, 0)
+    lax.fori_loop(0, blocks, step, 0)
+    for block in range(blocks):
+        out_copy(block).wait()
 
 
 def register_kernel(got_ref, hot_ref, out_ref, z_ref):
@@ -547,18 +608,21 @@
 
 
 VM = pl.BlockSpec(memory_space=pltpu.VMEM)
-SM = pl.BlockSpec(memory_space=pltpu.SMEM)
-
-
-def call(body, name, ins, outs, scratch=(), cost=0, limit=24):
+HB = pl.BlockSpec(memory_space=pltpu.HBM)
+
+
+LIMITS = (65472, 60 * 1024, 16384, 16384, 16384, 16384, 16384)
+
+
+def call(body, name, ins, outs, out_specs, scratch=(), cost=0, limit=16):
     return pl.pallas_call(
         body,
         name=name,
         in_specs=list(ins),
-        out_specs=[VM] * len(outs) if len(outs) > 1 else VM,
-        out_shape=outs if len(outs) > 1 else outs[0],
+        out_specs=list(out_specs),
+        out_shape=list(outs),
         scratch_shapes=list(scratch),
-        compiler_params=pltpu.CompilerParams(vmem_limit_bytes=limit << 20),
+        compiler_params=pltpu.CompilerParams(vmem_limit_bytes=limit << 10),
         cost_estimate=pl.CostEstimate(flops=cost, bytes_accessed=cost, transcendentals=0),
     )
 
@@ -575,6 +639,7 @@
     capacity = max(4, 2 * pieces // members)
     slots = members * capacity
     chunks = x_cells * PS // LANES
+    blocks = y_cells // ROWS
     patch_y = y_cells // PS
     assert chunks == PS and boxes == LANES and slots <= LANES and PS == QS
     assert y_cells == 4 * ROWS and pieces == SIDES * patch_y * (x_cells // PS)
@@ -582,90 +647,119 @@
     rows_all = NF * QUANT * CF
     wide = SIDES * patch_y * LANES
     count = pltpu.SMEM((members,), I32)
-
-    msg, low_edge, high_edge = call(
+    piece_list = pltpu.SMEM((pieces,), I32)
+    dma = pltpu.SemaphoreType.DMA
+    fine_shape = fine_state.shape
+    vmem = lambda *shape: pltpu.VMEM(shape, F32)
+    owners = piece_owner.reshape(pieces)
+
+    msg_shape = (members, (NF + 1) * ROWS, LANES)
+    edge_shape = (NF, edge_rows, LANES)
+    msg, low_edge, high_edge, code = call(
         functools.partial(prep_kernel, members, capacity, boxes),
         "prep",
-        (SM, SM, VM),
+        (HB, HB, HB),
         [
-            shaped(members, (NF + 1) * ROWS, LANES),
-            shaped(NF, edge_rows, LANES),
-            shaped(NF, edge_rows, LANES),
+            shaped(*msg_shape), shaped(*edge_shape), shaped(*edge_shape),
+            shaped(SIDES * patch_y, ROWS, LANES, dtype=I32),
         ],
-        [count],
+        (HB, HB, HB, VM),
+        [
+            piece_list, piece_list, count,
+            vmem(NF, ROWS, fine_shape[2]), vmem(NF, ROWS, fine_shape[2]),
+            vmem(NF, y_cells, LANES), vmem(NF, y_cells, LANES),
+            vmem(*msg_shape), vmem(*edge_shape), vmem(*edge_shape),
+            dma((6,)), dma((3,)),
+        ],
         cost=1 << 18,
-    )(piece_owner, piece_box, fine_state)
+        limit=LIMITS[0],
+    )(owners, piece_box, fine_state)
     got = lax.all_to_all(msg, "dev", split_axis=0, concat_axis=0, tiled=True)
     up = [(g, (g + 1) % groups) for g in range(groups)]
     down = [(b, a) for a, b in up]
     y_low = lax.ppermute(high_edge, "group", up)
     y_high = lax.ppermute(low_edge, "group", down)
 
-    wn, wz, zc, table, hot_fine = call(
-        functools.partial(build_kernel, members, capacity),
+    wz, table = call(
+        build_kernel,
         "build",
-        (SM, VM, VM),
+        (VM, HB),
+        [shaped(NF, PS, y_cells, LANES), shaped(TABLE_PAD, SIDES * boxes)],
+        (VM, VM),
         [
-            shaped(NF, chunks, y_cells, LANES),
-            shaped(NF, PS, y_cells, LANES),
-            shaped(NF, PS - 2, y_cells, LANES),
-            shaped(3, TABLE_PAD, SIDES * boxes, dtype=BF16),
-            shaped(CF * slots, wide, dtype=BF16),
-        ],
-        [
-            count,
-            pltpu.VMEM((NF, CB * CB * CB, boxes), F32),
+            vmem(NF, chunks, ROWS, LANES),
+            vmem(NF, boxes, CB * CB * CB),
+            vmem(NF, CB * CB * CB, boxes),
+            dma((NF,)),
         ],
         cost=1 << 23,
-    )(piece_owner, fine_state, coarse_boxes)
-
+        limit=LIMITS[1],
+    )(fine_state, coarse_boxes.transpose(1, 0, 2))
+
+    got, y_low, y_high = lax.optimization_barrier((got, y_low, y_high))
     payload, hot_box = call(
         serve_kernel,
         "serve",
         (VM, VM),
         [shaped(slots, TABLE_PAD), shaped(slots, SIDES * boxes, dtype=BF16)],
+        (HB, VM),
+        [vmem(slots, TABLE_PAD), dma((1,))],
         cost=1 << 18,
+        limit=LIMITS[2],
     )(got, table)
     back = lax.all_to_all(payload, "dev", split_axis=0, concat_axis=0, tiled=True)
 
-    plane = call(
+    (plane,) = call(
         functools.partial(plane_kernel, members),
         "plane",
-        (VM, VM, VM, VM),
+        (VM, VM, VM, VM, VM),
         [shaped(NF, chunks, y_cells, LANES)],
+        (VM,),
+        [vmem(NF, chunks, y_cells, LANES)],
         cost=1 << 24,
-    )(got, y_low, y_high, wn)
+        limit=LIMITS[3],
+    )(got, y_low, y_high, fine_state, hot_box)
 
     terms, edge = call(
         functools.partial(face_kernel, slots),
         "face",
         (VM, VM, VM, VM),
         [shaped(slots, LANES), shaped(NF, 4, y_cells, LANES)],
+        (HB, VM),
         [
-            pltpu.VMEM((TABLE_PAD, slots), F32),
-            pltpu.VMEM((rows_all, CF * slots), F32),
-            pltpu.VMEM((rows_all, wide), F32),
-            pltpu.VMEM((SIDES, NF, y_cells, LANES), F32),
-            pltpu.VMEM((TERM_ROWS, wide), F32),
+            pltpu.VMEM((CF * slots, wide), BF16),
+            vmem(TABLE_PAD, slots),
+            vmem(rows_all, CF * slots),
+            vmem(rows_all, wide),
+            vmem(SIDES, NF, y_cells, LANES),
+            vmem(TERM_ROWS, wide),
+            vmem(slots, LANES),
+            dma((1,)),
         ],
         cost=1 << 20,
-    )(back, hot_fine, wz, zc)
+        limit=LIMITS[4],
+    )(back, code, wz, plane)
     incoming = lax.all_to_all(terms, "dev", split_axis=0, concat_axis=0, tiled=True)
 
-    fine_next = call(
+    (fine_next,) = call(
         final_kernel,
         "final",
-        (VM, VM, VM, VM),
-        [shaped(*fine_state.shape)],
+        (VM, VM, VM),
+        [shaped(*fine_shape)],
+        (HB,),
+        [vmem(NF, PS - 2, ROWS, LANES), vmem(*fine_shape), dma((blocks,))],
         cost=1 << 23,
-    )(fine_state, plane, zc, edge)
-    flux_register = call(
+        limit=LIMITS[5],
+    )(wz, plane, edge)
+    (flux_register,) = call(
         register_kernel,
         "register",
         (VM, VM),
         [shaped(NF, SIDES * CF * CF, boxes)],
-        [pltpu.VMEM((LANES, SIDES * boxes), F32)],
+        (VM,),
+        [vmem(LANES, SIDES * boxes)],
         cost=1 << 18,
+        limit=LIMITS[6],
     )(incoming, hot_box)
     return (fine_next, flux_register)
 

time: 57.3 us -> 43.7 us (0.76)
  local copies, waits for them, and re-layouts: 10.3 us -> 2.31 us
  Pallas kernels: 27.7 us -> 21.3 us
  starting transfers between devices: 16.5 us -> 17.5 us
    unnamed x22 -> x10, local copies, waits for them, and re-layouts: 10.3 us -> 2.31 us
    pallas_call x4, Pallas kernels: 24.8 us -> 17.7 us  [the longest x1 6.05 us: local(): call(functools.partial(plane_kernel, members), 'plane', (VM, VM, VM, VM,...]
    all_to_all x1, waiting for transfers between devices: 1.37 us -> 0.01 us  [local(): lax.all_to_all(payload, 'dev', split_axis=0, concat_axis=0, tiled=True)]
    all_to_all x1, waiting for transfers between devices: 0.01 us -> 1.36 us  [local(): lax.all_to_all(terms, 'dev', split_axis=0, concat_axis=0, tiled=True)]
    all_to_all x1, starting transfers between devices: 3.32 us -> 4.21 us  [local(): lax.all_to_all(terms, 'dev', split_axis=0, concat_axis=0, tiled=True)]
    pallas_call x1, Pallas kernels: 0.33 us -> 0.99 us  [local(): call(serve_kernel, 'serve', (VM, VM), [shaped(slots, TABLE_PAD), shaped(s...]
  transfers between devices with their start and end apart: 5 -> 5, of which waited for: 1 -> 1; matrix products, arithmetic and copies ran while one was open for 4% -> 0% of each run, Pallas kernels for 44% -> 35%
where the time goes in v2:
time: 43.7 us; the launch traced here: 43.2 us
  Pallas kernels  21.3 us (49%)
  starting transfers between devices  17.5 us (40%)
  local copies, waits for them, and re-layouts  2.31 us (5%)
  waiting for transfers between devices  1.37 us (3%)
  between operations  0.75 us (2%)
    pallas_call x1, Pallas kernels, local(): call(functools.partial(plane_kernel, members), 'plane', (VM, VM, VM, VM,...  6.05 us
    pallas_call x1, Pallas kernels, local(): call(build_kernel, 'build', (VM, HB), [shaped(NF, PS, y_cells, LANES), sh...  5.7 us
    all_to_all x1, starting transfers between devices, local(): got = lax.all_to_all(msg, 'dev', split_axis=0, concat_axis=0, tiled=True)  5.21 us
    all_to_all x1, starting transfers between devices, local(): lax.all_to_all(payload, 'dev', split_axis=0, concat_axis=0, tiled=True)  4.21 us
    all_to_all x1, starting transfers between devices, local(): lax.all_to_all(terms, 'dev', split_axis=0, concat_axis=0, tiled=True)  4.21 us
    pallas_call x1, Pallas kernels, local(): call(final_kernel, 'final', (VM, VM, VM), [shaped(*fine_shape)], (HB,), [...  3.47 us
    pallas_call x1, Pallas kernels, local(): call(functools.partial(prep_kernel, members, capacity, boxes), 'prep', (H...  2.52 us
    unnamed x10, local copies, waits for them, and re-layouts  2.31 us
  transfers between devices with their start and end apart: 5, of which 1 were waited for; matrix products, arithmetic and copies ran while one was open for 0% of the time, Pallas kernels for 35%

profile of v2, /device:TPU:0, one launch (start us, length us, event | category | flops | bytes accessed | tf_op | source)
XLA Modules:
  0.0 43.2 jit_solution(18310945711761779675)
XLA Ops:
  0.6 2.5 %prep.1 = (f32[8,48,128]{2,1,0:T(8,128)}, f32[5,32,128]{2,1,0:T(8,128)}, f32[5,32,128]{2,1,0:T(8,128)}, s32[4,8,128]{2,1,0:T(8,128)}) custom-call(s32[32]{0:T(128)} %bitcast.9, s32[32]{0:T(128)} %box_hbm.1, f32[5,32,2048]{2,1,0:T(8,128)} %fine_ref.3), custom_call_target="tpu_custom_call" | custom-call | flops 262144 | bytes 262144 | tf_op jit(solution)/shard_map/prep/pallas_call | solution.py:658
  3.2 5.2 %all-to-all-start = ((f32[8,48,128]{2,1,0:T(8,128)}), f32[8,48,128]{2,1,0:T(8,128)S(1)}, u32[]{:S(2)}, u32[]{:S(2)}) async-start(f32[8,48,128]{2,1,0:T(8,128)} %get-tuple-element.16), calls=%async_computation | async-start | bytes 393216 | tf_op jit(solution)/shard_map/all_to_all | solution.py:677
  8.4 1.6 %collective-permute-start = (f32[5,32,128]{2,1,0:T(8,128)}, f32[5,32,128]{2,1,0:T(8,128)S(1)}, u32[]{:S(2)}, u32[]{:S(2)}) collective-permute-start(f32[5,32,128]{2,1,0:T(8,128)} %get-tuple-element.17), channel_id=1, source_target_pairs={{0,8},{8,16},{16,24},{24,0},{1,9},{9,17},{17,25},{25,1},{2,10},{10... | collective-permute-start | bytes 245768 | tf_op jit(solution)/shard_map/ppermute | solution.py:680
  9.9 2.2 %collective-permute-start.1 = (f32[5,32,128]{2,1,0:T(8,128)}, f32[5,32,128]{2,1,0:T(8,128)S(1)}, u32[]{:S(2)}, u32[]{:S(2)}) collective-permute-start(f32[5,32,128]{2,1,0:T(8,128)} %get-tuple-element.18), channel_id=1, source_target_pairs={{8,0},{16,8},{24,16},{0,24},{9,1},{17,9},{25,17},{1,25},{10,2},{18... | collective-permute-start | bytes 245768 | tf_op jit(solution)/shard_map/ppermute | solution.py:681
  12.2 0.0 copy-start
  12.2 5.7 %build.1 = (f32[5,16,32,128]{3,2,1,0:T(8,128)}, f32[384,256]{1,0:T(8,128)}) custom-call(f32[5,32,2048]{2,1,0:T(8,128)} %fine_ref.3, f32[5,128,512]{2,1,0:T(8,128)} %bitcast.8), custom_call_target="tpu_custom_call" | custom-call | flops 8388608 | bytes 8388608 | tf_op jit(solution)/shard_map/build/pallas_call | solution.py:683
  17.9 0.0 collective-permute-done.lo_ref
  17.9 0.0 collective-permute-done.1.hi_ref
  17.9 0.0 all-to-all-done.msg_ref
  17.9 0.0 copy-start.3
  17.9 1.0 %copy-done.3 = f32[384,256]{1,0:T(8,128)S(1)} copy-done((f32[384,256]{1,0:T(8,128)S(1)}, f32[384,256]{1,0:T(8,128)}, u32[]{:S(2)}) %copy-start.3) | copy-done | bytes 393240
  18.9 1.0 %serve.1 = (f32[64,384]{1,0:T(8,128)}, bf16[64,256]{1,0:T(8,128)(2,1)S(1)}) custom-call(f32[8,48,128]{2,1,0:T(8,128)S(1)} %all-to-all-done.msg_ref, f32[384,256]{1,0:T(8,128)S(1)} %copy-done.3), custom_call_target="tpu_custom_call" | custom-call | flops 262144 | bytes 262144 | tf_op jit(solution)/shard_map/serve/pallas_call | solution.py:700
  19.9 4.2 %all-to-all-start.1 = ((f32[8,8,384]{2,1,0:T(8,128)}), f32[8,8,384]{2,1,0:T(8,128)S(1)}, u32[]{:S(2)}, u32[]{:S(2)}) async-start(f32[8,8,384]{2,1,0:T(8,128)} %bitcast.2), calls=%async_computation.1 | async-start | bytes 196608 | tf_op jit(solution)/shard_map/all_to_all | solution.py:710
  24.1 0.0 copy-done
  24.1 0.0 copy-start.4
  24.1 6.0 %plane.1.after_ref.plane_ref = f32[5,16,32,128]{3,2,1,0:T(8,128)S(1)} custom-call(f32[8,48,128]{2,1,0:T(8,128)S(1)} %all-to-all-done.msg_ref, f32[5,32,128]{2,1,0:T(8,128)S(1)} %collective-permute-done.lo_ref, f32[5,32,128]{2,1,0:T(8,128)S(1)} %collective-permute-done.1.hi_ref, f32[5,32,2048]{2,1,0:T(8,128)S(1)} %copy-done, ...), custom_call_target="tpu_custom_call" | custom-call | flops 16777216 | bytes 16777216 | tf_op jit(solution)/shard_map/plane/pallas_call | solution.py:712
  30.2 0.0 all-to-all-done.1
  30.2 0.0 copy-done.4
  30.2 0.0 copy-start.1
  30.2 1.3 %copy-done.1 = f32[5,16,32,128]{3,2,1,0:T(8,128)S(1)} copy-done((f32[5,16,32,128]{3,2,1,0:T(8,128)S(1)}, f32[5,16,32,128]{3,2,1,0:T(8,128)}, u32[]{:S(2)}) %copy-start.1) | copy-done | bytes 1310744
  31.5 0.0 copy-start.2
  31.5 1.7 %face.1 = (f32[64,128]{1,0:T(8,128)}, f32[5,4,32,128]{3,2,1,0:T(8,128)S(1)}) custom-call(f32[64,384]{1,0:T(8,128)S(1)} %bitcast.6, s32[4,8,128]{2,1,0:T(8,128)S(1)} %copy-done.4, f32[5,16,32,128]{3,2,1,0:T(8,128)S(1)} %copy-done.1, f32[5,16,32,128]{3,2,1,0:T(8,128)S(1)} %plane.1.after_ref.plane_ref), custom_call_target="tpu_custom_call" | custom-call | flops 1048576 | bytes 1048576 | tf_op jit(solution)/shard_map/face/pallas_call | solution.py:723
  33.3 4.2 %all-to-all-start.2 = ((f32[8,8,128]{2,1,0:T(8,128)}), f32[8,8,128]{2,1,0:T(8,128)S(1)}, u32[]{:S(2)}, u32[]{:S(2)}) async-start(f32[8,8,128]{2,1,0:T(8,128)} %bitcast.4), calls=%async_computation.2 | async-start | bytes 65536 | tf_op jit(solution)/shard_map/all_to_all | solution.py:742
  37.5 0.0 copy-done.2
  37.5 3.5 %final.1 = f32[5,32,2048]{2,1,0:T(8,128)} custom-call(f32[5,16,32,128]{3,2,1,0:T(8,128)S(1)} %copy-done.2, f32[5,16,32,128]{3,2,1,0:T(8,128)S(1)} %plane.1.after_ref.plane_ref, f32[5,4,32,128]{3,2,1,0:T(8,128)S(1)} %get-tuple-element.26.edge_ref), custom_call_target="tpu_custom_call" | custom-call | flops 8388608 | bytes 8388608 | tf_op jit(solution)/shard_map/final/pallas_call | solution.py:744
  40.9 1.4 %all-to-all-done.2 = f32[8,8,128]{2,1,0:T(8,128)S(1)} async-done(((f32[8,8,128]{2,1,0:T(8,128)}), f32[8,8,128]{2,1,0:T(8,128)S(1)}, u32[]{:S(2)}, u32[]{:S(2)}) %all-to-all-start.2) | async-done | bytes 32800 | tf_op jit(solution)/shard_map/all_to_all | solution.py:742
  42.3 0.9 %register.1 = f32[5,32,128]{2,1,0:T(8,128)} custom-call(f32[64,128]{1,0:T(8,128)S(1)} %bitcast.7, bf16[64,256]{1,0:T(8,128)(2,1)S(1)} %get-tuple-element.23.after_ref.hot_ref), custom_call_target="tpu_custom_call" | custom-call | flops 262144 | bytes 262144 | tf_op jit(solution)/shard_map/register/pallas_call | solution.py:754
Async XLA Ops:
  3.2 14.8 %all-to-all-start = ((f32[8,48,128]{2,1,0:T(8,128)}), f32[8,48,128]{2,1,0:T(8,128)S(1)}, u32[]{:S(2)}, u32[]{:S(2)}) async-start(f32[8,48,128]{2,1,0:T(8,128)} %get-tuple-element.16), calls=%async_computation | async-start | bytes 393216 | tf_op jit(solution)/shard_map/all_to_all | solution.py:677
  8.4 9.5 %collective-permute-start = (f32[5,32,128]{2,1,0:T(8,128)}, f32[5,32,128]{2,1,0:T(8,128)S(1)}, u32[]{:S(2)}, u32[]{:S(2)}) collective-permute-start(f32[5,32,128]{2,1,0:T(8,128)} %get-tuple-element.17), channel_id=1, source_target_pairs={{0,8},{8,16},{16,24},{24,0},{1,9},{9,17},{17,25},{25,1},{2,10},{10... | collective-permute-start | bytes 245768 | tf_op jit(solution)/shard_map/ppermute | solution.py:680
  9.9 8.0 %collective-permute-start.1 = (f32[5,32,128]{2,1,0:T(8,128)}, f32[5,32,128]{2,1,0:T(8,128)S(1)}, u32[]{:S(2)}, u32[]{:S(2)}) collective-permute-start(f32[5,32,128]{2,1,0:T(8,128)} %get-tuple-element.18), channel_id=1, source_target_pairs={{8,0},{16,8},{24,16},{0,24},{9,1},{17,9},{25,17},{1,25},{10,2},{18... | collective-permute-start | bytes 245768 | tf_op jit(solution)/shard_map/ppermute | solution.py:681
  12.2 11.9 %copy-start = (f32[5,32,2048]{2,1,0:T(8,128)S(1)}, f32[5,32,2048]{2,1,0:T(8,128)}, u32[]{:S(2)}) copy-start(f32[5,32,2048]{2,1,0:T(8,128)} %fine_ref.3) | copy-start | bytes 3932164
  17.9 1.0 %copy-start.3 = (f32[384,256]{1,0:T(8,128)S(1)}, f32[384,256]{1,0:T(8,128)}, u32[]{:S(2)}) copy-start(f32[384,256]{1,0:T(8,128)} %get-tuple-element.22.tab_ref) | copy-start | bytes 1179652
  19.9 10.3 %all-to-all-start.1 = ((f32[8,8,384]{2,1,0:T(8,128)}), f32[8,8,384]{2,1,0:T(8,128)S(1)}, u32[]{:S(2)}, u32[]{:S(2)}) async-start(f32[8,8,384]{2,1,0:T(8,128)} %bitcast.2), calls=%async_computation.1 | async-start | bytes 196608 | tf_op jit(solution)/shard_map/all_to_all | solution.py:710
  24.1 6.1 %copy-start.4 = (s32[4,8,128]{2,1,0:T(8,128)S(1)}, s32[4,8,128]{2,1,0:T(8,128)}, u32[]{:S(2)}) copy-start(s32[4,8,128]{2,1,0:T(8,128)} %get-tuple-element.25.code_ref) | copy-start | bytes 49156
  30.2 1.3 %copy-start.1 = (f32[5,16,32,128]{3,2,1,0:T(8,128)S(1)}, f32[5,16,32,128]{3,2,1,0:T(8,128)}, u32[]{:S(2)}) copy-start(f32[5,16,32,128]{3,2,1,0:T(8,128)} %get-tuple-element.15.wz_ref) | copy-start | bytes 3932164
  31.5 5.9 %copy-start.2 = (f32[5,16,32,128]{3,2,1,0:T(8,128)S(1)}, f32[5,16,32,128]{3,2,1,0:T(8,128)}, u32[]{:S(2)}) copy-start(f32[5,16,32,128]{3,2,1,0:T(8,128)} %get-tuple-element.15.wz_ref) | copy-start | bytes 3932164
  33.3 9.0 %all-to-all-start.2 = ((f32[8,8,128]{2,1,0:T(8,128)}), f32[8,8,128]{2,1,0:T(8,128)S(1)}, u32[]{:S(2)}, u32[]{:S(2)}) async-start(f32[8,8,128]{2,1,0:T(8,128)} %bitcast.4), calls=%async_computation.2 | async-start | bytes 65536 | tf_op jit(solution)/shard_map/all_to_all | solution.py:742

commit v3 on v2

--- a/solution.py
+++ b/solution.py
@@ -6,6 +6,7 @@
 from jax.experimental import pallas as pl
 from jax.experimental.pallas import tpu as pltpu
 from jax.sharding import PartitionSpec as P
+
 
 PS = 16
 RATIO = 4
@@ -25,6 +26,8 @@
 TABLE_ROWS = NF * QUANT * CF * CF
 TABLE_PAD = 384
 TERM_ROWS = 32
+Y_EARLY = 1
+NEAR = 3
 
 
 def iota(shape, dim):
@@ -191,7 +194,9 @@
         copy.wait()
 
 
-def build_kernel(fine_ref, coarse_hbm, wz_ref, tab_ref, wn_ref, cs_ref, ct_ref, coarse_sem):
+def build_kernel(
+    fine_ref, coarse_hbm, wz_hbm, tab_ref, wn_ref, wz_ref, cs_ref, ct_ref, coarse_sem, wz_sem
+):
     chunks = fine_ref.shape[2] // LANES
     blocks = fine_ref.shape[1] // ROWS
     coarse_copies = [
@@ -200,7 +205,6 @@
     for copy in coarse_copies:
         copy.start()
     lane = iota((ROWS, LANES), 1)
-    sub = iota((ROWS, LANES), 0)
 
     def turn(block, carry):
         rows = pl.ds(pl.multiple_of(block * ROWS, ROWS), ROWS)
@@ -217,14 +221,15 @@
         return carry
 
     lax.fori_loop(0, blocks, turn, 0)
-
+    wz_copy = pltpu.make_async_copy(wz_ref, wz_hbm, wz_sem.at[0])
+    wz_copy.start()
+    sub = iota((ROWS, LANES), 0)
     boxes = coarse_hbm.shape[1]
     for f in range(NF):
         coarse_copies[f].wait()
         for j in range(CB * CB * CB // LANES):
             at = slice(j * LANES, (j + 1) * LANES)
             ct_ref[f, at, :] = cs_ref[f, :, at].T
-    tab_ref[TABLE_ROWS:, :] = jnp.zeros((TABLE_PAD - TABLE_ROWS, SIDES * boxes), F32)
     for s in range(SIDES):
         middle = CB - 3 if s == 0 else 2
 
@@ -254,6 +259,7 @@
                             pltpu.roll(found[f, q, 2 * i + 1], 2, 0),
                         )
                     )
+    wz_copy.wait()
 
 
 def serve_kernel(msg_ref, tab_ref, out_hbm, hot_ref, out_ref, sem_ref):
@@ -274,7 +280,8 @@
             hot, part, (((1,), (1,)), ((), ())), preferred_element_type=F32
         )
         total = got if total is None else total + got
-    out_ref[...] = total
+    out_ref[:, 0:TABLE_ROWS] = total
+    out_ref[:, TABLE_ROWS:] = jnp.zeros((slot_count, TABLE_PAD - TABLE_ROWS), F32)
     copy = pltpu.make_async_copy(out_ref, out_hbm, sem_ref.at[0])
     copy.start()
     copy.wait()
@@ -310,14 +317,75 @@
         low_moved = low_next
 
 
+def y_columns(j, skip, blocks, lo_ref, hi_ref, load, add):
+    sub = iota((ROWS, LANES), 0)
+
+    def y_back(before, here):
+        if before is None:
+            return pltpu.roll(here, 1, 0)
+        return jnp.where(sub < 1, before, here)
+
+    def y_forward(here, after):
+        if here is None:
+            return pltpu.roll(after, ROWS - 1, 0)
+        return jnp.where(sub >= ROWS - 1, after, here)
+
+    ends = []
+    for k in range(ROWS):
+        at = slice((2 * (j - skip) + k // 4) * ROWS, (2 * (j - skip) + k // 4 + 1) * ROWS)
+        if k % 4 == 0:
+            low = to_primitive([lo_ref[f, at, :] for f in range(NF)])
+            high = to_primitive([hi_ref[f, at, :] for f in range(NF)])
+        c = ROWS * j + k
+        turn_low, turn_high = (6 - 2 * (k % 4)) % ROWS, (ROWS - 2 * (k % 4)) % ROWS
+        below = [pltpu.roll(t, turn_low, 0) if turn_low else t for t in low]
+        above = [pltpu.roll(t, turn_high, 0) if turn_high else t for t in high]
+        tiles = [load(c, b) for b in range(blocks)]
+
+        def emit(b, change):
+            for f in range(NF):
+                add(f, c, b, change[f])
+
+        sweep_line(
+            [below] + tiles + [above], 1, y_back, y_forward, emit, lambda *end: ends.append(end)
+        )
+    packed = []
+    for which in range(2):
+        state = []
+        for f in range(NF):
+            tile = ends[0][which][f]
+            for k in range(1, ROWS):
+                tile = jnp.where(sub == k, pltpu.roll(ends[k][which][f], k, 0), tile)
+            state.append(tile)
+        packed.append(state)
+    top = hll(packed[0], packed[1], 1)
+    for k in range(ROWS):
+        c = ROWS * j + k
+        flux, flux_moved = ends[k][2], ends[k][3]
+        for f in range(NF):
+            moved = pltpu.roll(top[f], ROWS - 1 - k, 0) if k < ROWS - 1 else top[f]
+            change = y_forward(flux_moved[f], moved) - flux[f]
+            add(f, c, blocks - 1, change)
+
+
 def plane_kernel(
-    members, msg_ref, lo_ref, hi_ref, fine_ref, after_ref, out_ref, wn_ref
+    members, msg_ref, lo_ref, hi_ref, fine_ref, after_ref, wz_hbm,
+    out_ref, near_ref, ends_ref, wn_ref, sem_ref,
 ):
+    near_copies = [
+        pltpu.make_async_copy(
+            wz_hbm.at[:, start : start + NEAR],
+            near_ref.at[:, i * NEAR : (i + 1) * NEAR],
+            sem_ref.at[i],
+        )
+        for i, start in enumerate((0, PS - NEAR))
+    ]
+    for copy in near_copies:
+        copy.start()
     me = lax.axis_index("dev")
     chunks = fine_ref.shape[2] // LANES
     blocks = fine_ref.shape[1] // ROWS
     lane = iota((ROWS, LANES), 1)
-    sub = iota((ROWS, LANES), 0)
     width = 2 * PS
     place = jnp.full((ROWS, LANES), me, I32)
 
@@ -371,71 +439,30 @@
 
     lax.fori_loop(0, blocks, x_block, 0)
 
-    def y_back(before, here):
-        if before is None:
-            return pltpu.roll(here, 1, 0)
-        return jnp.where(sub < 1, before, here)
-
-    def y_forward(here, after):
-        if here is None:
-            return pltpu.roll(after, ROWS - 1, 0)
-        return jnp.where(sub >= ROWS - 1, after, here)
-
-    def y_block(j, carry):
-        ends = []
-        for k in range(ROWS):
-            at = pl.ds(pl.multiple_of((2 * j + k // 4) * ROWS, ROWS), ROWS)
-            if k % 4 == 0:
-                low = to_primitive([lo_ref[f, at, :] for f in range(NF)])
-                high = to_primitive([hi_ref[f, at, :] for f in range(NF)])
-            c = ROWS * j + k
-            turn_low, turn_high = (6 - 2 * (k % 4)) % ROWS, (ROWS - 2 * (k % 4)) % ROWS
-            below = [pltpu.roll(t, turn_low, 0) if turn_low else t for t in low]
-            above = [pltpu.roll(t, turn_high, 0) if turn_high else t for t in high]
-            tiles = [
-                [wn_ref[f, c, b * ROWS : (b + 1) * ROWS, :] for f in range(NF)]
-                for b in range(blocks)
-            ]
-
-            def emit(b, change):
-                at = slice(b * ROWS, (b + 1) * ROWS)
-                for f in range(NF):
-                    out_ref[f, c, at, :] = out_ref[f, c, at, :] - DT_DX * change[f]
-
-            sweep_line(
-                [below] + tiles + [above], 1, y_back, y_forward, emit, lambda *end: ends.append(end)
-            )
-        packed = []
-        for which in range(2):
-            state = []
-            for f in range(NF):
-                tile = ends[0][which][f]
-                for k in range(1, ROWS):
-                    tile = jnp.where(sub == k, pltpu.roll(ends[k][which][f], k, 0), tile)
-                state.append(tile)
-            packed.append(state)
-        top = hll(packed[0], packed[1], 1)
-        at = slice((blocks - 1) * ROWS, blocks * ROWS)
-        for k in range(ROWS):
-            c = ROWS * j + k
-            flux, flux_moved = ends[k][2], ends[k][3]
-            for f in range(NF):
-                moved = pltpu.roll(top[f], ROWS - 1 - k, 0) if k < ROWS - 1 else top[f]
-                change = y_forward(flux_moved[f], moved) - flux[f]
-                out_ref[f, c, at, :] = out_ref[f, c, at, :] - DT_DX * change
-        return carry
-
-    lax.fori_loop(0, chunks // ROWS, y_block, 0)
+    def load(c, b):
+        return [wn_ref[f, c, b * ROWS : (b + 1) * ROWS, :] for f in range(NF)]
+
+    def add(f, c, b, change):
+        at = slice(b * ROWS, (b + 1) * ROWS)
+        out_ref[f, c, at, :] = out_ref[f, c, at, :] - DT_DX * change
+
+    first = 2 * ROWS * Y_EARLY
+    ends_ref[0] = lo_ref[:, first:, :]
+    ends_ref[1] = hi_ref[:, first:, :]
+    for j in range(Y_EARLY):
+        y_columns(j, 0, blocks, lo_ref, hi_ref, load, add)
+    for copy in near_copies:
+        copy.wait()
 
 
 def face_kernel(
-    slot_count, got_ref, code_ref, wz_ref, after_ref, term_hbm, edge_ref,
-    he_ref, rt_ref, lf_ref, g_ref, fs_ref, v_ref, term_ref, sem_ref,
+    slot_count, got_ref, code_ref, near_ref, after_ref, term_hbm, edge_hbm,
+    edge_ref, he_ref, rt_ref, lf_ref, g_ref, fs_ref, v_ref, term_ref, sem_ref,
 ):
     lane = iota((ROWS, LANES), 1)
     sub = iota((ROWS, LANES), 0)
     rows_all = NF * QUANT * CF
-    y_cells = wz_ref.shape[2]
+    y_cells = near_ref.shape[2]
     blocks = y_cells // ROWS
     patch_y = y_cells // PS
     number = iota((CF * slot_count, LANES), 0)
@@ -485,8 +512,7 @@
                     )
 
             inner = [
-                [wz_ref[f, z, rows, :] for f in range(NF)]
-                for z in (range(3) if s == 0 else range(PS - 3, PS))
+                [near_ref[f, NEAR * s + i, rows, :] for f in range(NF)] for i in range(NEAR)
             ]
             line = ghosts + inner if s == 0 else inner + ghosts
             diff = [[line[i + 1][f] - line[i][f] for f in range(NF)] for i in range(4)]
@@ -511,6 +537,8 @@
                     edge_ref[f, 3, rows, :] = flux[1][f] - flux[0][f]
                     fs_ref[1, f, rows, :] = flux[1][f]
 
+    edge_copy = pltpu.make_async_copy(edge_ref, edge_hbm, sem_ref.at[1])
+    edge_copy.start()
     v_ref[NF * CF :, :] = jnp.zeros((TERM_ROWS - NF * CF, v_ref.shape[1]), F32)
     for s in range(SIDES):
         for f in range(NF):
@@ -536,15 +564,23 @@
         ]
     copy = pltpu.make_async_copy(term_ref, term_hbm, sem_ref.at[0])
     copy.start()
+    edge_copy.wait()
     copy.wait()
 
 
 def final_kernel(
-    wz_ref, plane_ref, edge_ref, out_hbm, zc_ref, out_ref, out_sem
+    fine_ref, plane_ref, edge_hbm, ends_ref, wz_hbm, out_hbm,
+    edge_ref, wz_ref, zc_ref, extra_ref, out_ref, wz_sem, out_sem,
 ):
     lane = iota((ROWS, LANES), 1)
     chunks = plane_ref.shape[1]
     blocks = plane_ref.shape[2] // ROWS
+
+    def wz_copy(block):
+        rows = pl.ds(pl.multiple_of(block * ROWS, ROWS), ROWS)
+        return pltpu.make_async_copy(
+            wz_hbm.at[:, :, rows, :], wz_ref.at[:, :, rows, :], wz_sem.at[block]
+        )
 
     def out_copy(block):
         rows = pl.ds(pl.multiple_of(block * ROWS, ROWS), ROWS)
@@ -552,8 +588,28 @@
             out_ref.at[:, rows, :], out_hbm.at[:, rows, :], out_sem.at[block]
         )
 
+    edge_copy = pltpu.make_async_copy(edge_hbm, edge_ref, wz_sem.at[blocks])
+    edge_copy.start()
+    for block in range(blocks):
+        wz_copy(block).start()
+    first = Y_EARLY * ROWS
+
+    def load(c, b):
+        at = slice(b * ROWS, (b + 1) * ROWS)
+        return to_primitive([fine_ref[f, at, c * LANES : (c + 1) * LANES] for f in range(NF)])
+
+    def add(f, c, b, change):
+        at = slice(b * ROWS, (b + 1) * ROWS)
+        extra_ref[f, c - first, at, :] = plane_ref[f, c, at, :] - DT_DX * change
+
+    for j in range(Y_EARLY, chunks // ROWS):
+        y_columns(j, Y_EARLY, blocks, ends_ref.at[0], ends_ref.at[1], load, add)
+
+    edge_copy.wait()
+
     def step(block, carry):
         rows = pl.ds(pl.multiple_of(block * ROWS, ROWS), ROWS)
+        wz_copy(block).wait()
 
         def load(z):
             return [wz_ref[f, z, rows, :] for f in range(NF)]
@@ -583,11 +639,16 @@
             tiles = swap_groups(tiles, lane)
             for c in range(chunks):
                 at = slice(c * LANES, (c + 1) * LANES)
-                out_ref[f, rows, at] = plane_ref[f, c, rows, :] - DT_DX * tiles[c]
+                if c < first:
+                    partial = plane_ref[f, c, rows, :]
+                else:
+                    partial = extra_ref[f, c - first, rows, :]
+                out_ref[f, rows, at] = partial - DT_DX * tiles[c]
         out_copy(block).start()
         return carry
 
     lax.fori_loop(0, blocks, step, 0)
+
     for block in range(blocks):
         out_copy(block).wait()
 
@@ -611,20 +672,28 @@
 HB = pl.BlockSpec(memory_space=pltpu.HBM)
 
 
-LIMITS = (65472, 60 * 1024, 16384, 16384, 16384, 16384, 16384)
-
-
-def call(body, name, ins, outs, out_specs, scratch=(), cost=0, limit=16):
-    return pl.pallas_call(
+def call(body, ins, outs, out_specs, scratch=(), cost=0, limit=8 << 10):
+    kernel = pl.pallas_call(
         body,
-        name=name,
         in_specs=list(ins),
         out_specs=list(out_specs),
-        out_shape=list(outs),
+        out_shape=[
+            pltpu.HBM(o.shape, o.dtype) if spec is HB else o for o, spec in zip(outs, out_specs)
+        ],
         scratch_shapes=list(scratch),
         compiler_params=pltpu.CompilerParams(vmem_limit_bytes=limit << 10),
         cost_estimate=pl.CostEstimate(flops=cost, bytes_accessed=cost, transcendentals=0),
     )
+
+    def run(*args):
+        return kernel(
+            *[
+                pltpu.with_memory_space_constraint(a, pltpu.HBM) if spec is HB else a
+                for a, spec in zip(args, ins)
+            ]
+        )
+
+    return run
 
 
 def shaped(*shape, dtype=F32):
@@ -657,7 +726,6 @@
     edge_shape = (NF, edge_rows, LANES)
     msg, low_edge, high_edge, code = call(
         functools.partial(prep_kernel, members, capacity, boxes),
-        "prep",
         (HB, HB, HB),
         [
             shaped(*msg_shape), shaped(*edge_shape), shaped(*edge_shape),
@@ -672,7 +740,6 @@
             dma((6,)), dma((3,)),
         ],
         cost=1 << 18,
-        limit=LIMITS[0],
     )(owners, piece_box, fine_state)
     got = lax.all_to_all(msg, "dev", split_axis=0, concat_axis=0, tiled=True)
     up = [(g, (g + 1) % groups) for g in range(groups)]
@@ -680,53 +747,59 @@
     y_low = lax.ppermute(high_edge, "group", up)
     y_high = lax.ppermute(low_edge, "group", down)
 
-    wz, table = call(
+    turned_shape = (NF, PS, y_cells, LANES)
+    build = call(
         build_kernel,
-        "build",
         (VM, HB),
-        [shaped(NF, PS, y_cells, LANES), shaped(TABLE_PAD, SIDES * boxes)],
-        (VM, VM),
+        [
+            shaped(*turned_shape),
+            shaped(TABLE_ROWS, SIDES * boxes),
+        ],
+        (HB, VM),
         [
             vmem(NF, chunks, ROWS, LANES),
+            vmem(*turned_shape),
             vmem(NF, boxes, CB * CB * CB),
             vmem(NF, CB * CB * CB, boxes),
             dma((NF,)),
+            dma((1,)),
         ],
         cost=1 << 23,
-        limit=LIMITS[1],
-    )(fine_state, coarse_boxes.transpose(1, 0, 2))
-
-    got, y_low, y_high = lax.optimization_barrier((got, y_low, y_high))
+    )
+    wz, table = build(fine_state, coarse_boxes.transpose(1, 0, 2))
     payload, hot_box = call(
         serve_kernel,
-        "serve",
         (VM, VM),
         [shaped(slots, TABLE_PAD), shaped(slots, SIDES * boxes, dtype=BF16)],
         (HB, VM),
         [vmem(slots, TABLE_PAD), dma((1,))],
         cost=1 << 18,
-        limit=LIMITS[2],
     )(got, table)
     back = lax.all_to_all(payload, "dev", split_axis=0, concat_axis=0, tiled=True)
 
-    (plane,) = call(
+    plane, near, ends = call(
         functools.partial(plane_kernel, members),
-        "plane",
-        (VM, VM, VM, VM, VM),
-        [shaped(NF, chunks, y_cells, LANES)],
-        (VM,),
-        [vmem(NF, chunks, y_cells, LANES)],
+        (VM, VM, VM, VM, VM, HB),
+        [
+            shaped(NF, chunks, y_cells, LANES),
+            shaped(NF, 2 * NEAR, y_cells, LANES),
+            shaped(2, NF, edge_rows - 2 * ROWS * Y_EARLY, LANES),
+        ],
+        (VM, VM, VM),
+        [
+            vmem(NF, chunks, y_cells, LANES),
+            dma((2,)),
+        ],
         cost=1 << 24,
-        limit=LIMITS[3],
-    )(got, y_low, y_high, fine_state, hot_box)
+    )(got, y_low, y_high, fine_state, hot_box, wz)
 
     terms, edge = call(
         functools.partial(face_kernel, slots),
-        "face",
         (VM, VM, VM, VM),
         [shaped(slots, LANES), shaped(NF, 4, y_cells, LANES)],
-        (HB, VM),
+        (HB, HB),
         [
+            vmem(NF, 4, y_cells, LANES),
             pltpu.VMEM((CF * slots, wide), BF16),
             vmem(TABLE_PAD, slots),
             vmem(rows_all, CF * slots),
@@ -734,32 +807,35 @@
             vmem(SIDES, NF, y_cells, LANES),
             vmem(TERM_ROWS, wide),
             vmem(slots, LANES),
-            dma((1,)),
+            dma((2,)),
         ],
         cost=1 << 20,
-        limit=LIMITS[4],
-    )(back, code, wz, plane)
+    )(back, code, near, plane)
     incoming = lax.all_to_all(terms, "dev", split_axis=0, concat_axis=0, tiled=True)
 
     (fine_next,) = call(
         final_kernel,
-        "final",
-        (VM, VM, VM),
+        (VM, VM, HB, VM, HB),
         [shaped(*fine_shape)],
         (HB,),
-        [vmem(NF, PS - 2, ROWS, LANES), vmem(*fine_shape), dma((blocks,))],
-        cost=1 << 23,
-        limit=LIMITS[5],
-    )(wz, plane, edge)
+        [
+            vmem(NF, 4, y_cells, LANES),
+            vmem(*turned_shape),
+            vmem(NF, PS - 2, ROWS, LANES),
+            vmem(NF, chunks - Y_EARLY * ROWS, y_cells, LANES),
+            vmem(*fine_shape),
+            dma((blocks + 1,)),
+            dma((blocks,)),
+        ],
+        cost=1 << 24,
+    )(fine_state, plane, edge, ends, wz)
     (flux_register,) = call(
         register_kernel,
-        "register",
         (VM, VM),
         [shaped(NF, SIDES * CF * CF, boxes)],
         (VM,),
         [vmem(LANES, SIDES * boxes)],
         cost=1 << 18,
-        limit=LIMITS[6],
     )(incoming, hot_box)
     return (fine_next, flux_register)
 

time: 43.7 us -> 43.2 us (0.989)
  waiting for transfers between devices: 1.37 us -> 6.7 us
  Pallas kernels: 21.3 us -> 19 us
  local copies, waits for them, and re-layouts: 2.31 us -> 0.01 us
  starting transfers between devices: 17.5 us -> 16.3 us
    ppermute x1, waiting for transfers between devices: 0.01 us -> 3.01 us  [local(): y_low = lax.ppermute(high_edge, 'group', up)]
    all_to_all x1, waiting for transfers between devices: 0.01 us -> 2.52 us  [local(): got = lax.all_to_all(msg, 'dev', split_axis=0, concat_axis=0, tiled=True)]
    pallas_call x7, Pallas kernels: 21.3 us -> 19 us  [run(): kernel(*[pltpu.with_memory_space_constraint(a, pltpu.HBM) if spec is HB e...]
    unnamed x10 -> x6, local copies, waits for them, and re-layouts: 2.31 us -> 0.01 us
    all_to_all x1, waiting for transfers between devices: 1.36 us -> 0.26 us  [local(): lax.all_to_all(terms, 'dev', split_axis=0, concat_axis=0, tiled=True)]
    ppermute x1, waiting for transfers between devices: 0.01 us -> 0.91 us  [local(): y_high = lax.ppermute(low_edge, 'group', down)]
    all_to_all x1, starting transfers between devices: 4.21 us -> 3.37 us  [local(): lax.all_to_all(payload, 'dev', split_axis=0, concat_axis=0, tiled=True)]
  transfers between devices with their start and end apart: 5 -> 5, of which waited for: 1 -> 4; matrix products, arithmetic and copies ran while one was open for 0% -> 0% of each run, Pallas kernels for 35% -> 31%
where the time goes in v3:
time: 43.2 us; the launch traced here: 42.7 us
  Pallas kernels  19 us (44%)
  starting transfers between devices  16.3 us (38%)
  waiting for transfers between devices  6.7 us (16%)
  between operations  0.73 us (2%)
    pallas_call x7, Pallas kernels, run(): kernel(*[pltpu.with_memory_space_constraint(a, pltpu.HBM) if spec is HB e...  19 us
    all_to_all x1, starting transfers between devices, local(): got = lax.all_to_all(msg, 'dev', split_axis=0, concat_axis=0, tiled=True)  5.21 us
    all_to_all x1, starting transfers between devices, local(): lax.all_to_all(terms, 'dev', split_axis=0, concat_axis=0, tiled=True)  3.87 us
    all_to_all x1, starting transfers between devices, local(): lax.all_to_all(payload, 'dev', split_axis=0, concat_axis=0, tiled=True)  3.37 us
    ppermute x1, waiting for transfers between devices, local(): y_low = lax.ppermute(high_edge, 'group', up)  3.01 us
    all_to_all x1, waiting for transfers between devices, local(): got = lax.all_to_all(msg, 'dev', split_axis=0, concat_axis=0, tiled=True)  2.52 us
    ppermute x1, starting transfers between devices, local(): y_high = lax.ppermute(low_edge, 'group', down)  2.25 us
    ppermute x1, starting transfers between devices, local(): y_low = lax.ppermute(high_edge, 'group', up)  1.63 us
  transfers between devices with their start and end apart: 5, of which 4 were waited for; matrix products, arithmetic and copies ran while one was open for 0% of the time, Pallas kernels for 31%

profile of v3, /device:TPU:0, one launch (start us, length us, event | category | flops | bytes accessed | tf_op | source)
XLA Modules:
  0.0 42.7 jit_solution(17047786405493954661)
XLA Ops:
  0.6 0.0 copy-start
  0.6 2.0 %shard_map.59 = (f32[8,48,128]{2,1,0:T(8,128)}, f32[5,32,128]{2,1,0:T(8,128)}, f32[5,32,128]{2,1,0:T(8,128)}, s32[4,8,128]{2,1,0:T(8,128)S(1)}) custom-call(s32[32]{0:T(128)} %bitcast.11, s32[32]{0:T(128)} %box_hbm.1, f32[5,32,2048]{2,1,0:T(8,128)} %fine_ref.5), custom_call_target="tpu_custom_call" | custom-call | flops 262144 | bytes 262144 | tf_op jit(solution)/shard_map/pallas_call | solution.py:689
  2.7 5.2 %all-to-all-start = ((f32[8,48,128]{2,1,0:T(8,128)}), f32[8,48,128]{2,1,0:T(8,128)S(1)}, u32[]{:S(2)}, u32[]{:S(2)}) async-start(f32[8,48,128]{2,1,0:T(8,128)} %get-tuple-element.15), calls=%async_computation | async-start | bytes 393216 | tf_op jit(solution)/shard_map/all_to_all | solution.py:744
  7.9 0.0 copy-done
  7.9 0.0 copy-start.2
  7.9 0.0 copy-start.1
  7.9 3.6 %shard_map.60 = (f32[5,16,32,128]{3,2,1,0:T(8,128)}, f32[320,256]{1,0:T(8,128)S(1)}) custom-call(f32[5,32,2048]{2,1,0:T(8,128)S(1)} %copy-done, f32[5,128,512]{2,1,0:T(8,128)} %bitcast.8), custom_call_target="tpu_custom_call" | custom-call | flops 8388608 | bytes 8388608 | tf_op jit(solution)/shard_map/pallas_call | solution.py:689
  11.5 2.5 %all-to-all-done.msg_ref = f32[8,48,128]{2,1,0:T(8,128)S(1)} async-done(((f32[8,48,128]{2,1,0:T(8,128)}), f32[8,48,128]{2,1,0:T(8,128)S(1)}, u32[]{:S(2)}, u32[]{:S(2)}) %all-to-all-start) | async-done | bytes 196640 | tf_op jit(solution)/shard_map/all_to_all | solution.py:744
  14.1 1.0 %shard_map.61 = (f32[64,384]{1,0:T(8,128)}, bf16[64,256]{1,0:T(8,128)(2,1)S(1)}) custom-call(f32[8,48,128]{2,1,0:T(8,128)S(1)} %all-to-all-done.msg_ref, f32[320,256]{1,0:T(8,128)S(1)} %get-tuple-element.18.tab_ref), custom_call_target="tpu_custom_call" | custom-call | flops 262144 | bytes 262144 | tf_op jit(solution)/shard_map/pallas_call | solution.py:689
  15.0 3.4 %all-to-all-start.1 = ((f32[8,8,384]{2,1,0:T(8,128)}), f32[8,8,384]{2,1,0:T(8,128)S(1)}, u32[]{:S(2)}, u32[]{:S(2)}) async-start(f32[8,8,384]{2,1,0:T(8,128)} %bitcast.9), calls=%async_computation.1 | async-start | bytes 196608 | tf_op jit(solution)/shard_map/all_to_all | solution.py:778
  18.4 0.0 copy-done.2
  18.4 1.6 %collective-permute-start = (f32[5,32,128]{2,1,0:T(8,128)S(1)}, f32[5,32,128]{2,1,0:T(8,128)S(1)}, u32[]{:S(2)}, u32[]{:S(2)}) collective-permute-start(f32[5,32,128]{2,1,0:T(8,128)S(1)} %copy-done.2), channel_id=1, source_target_pairs={{0,8},{8,16},{16,24},{24,0},{1,9},{9,17},{17,25},{25,1},{2,10},{10... | collective-permute-start | bytes 245768 | tf_op jit(solution)/shard_map/ppermute | solution.py:747
  20.1 0.0 copy-done.1
  20.1 2.2 %collective-permute-start.1 = (f32[5,32,128]{2,1,0:T(8,128)S(1)}, f32[5,32,128]{2,1,0:T(8,128)S(1)}, u32[]{:S(2)}, u32[]{:S(2)}) collective-permute-start(f32[5,32,128]{2,1,0:T(8,128)S(1)} %copy-done.1), channel_id=1, source_target_pairs={{8,0},{16,8},{24,16},{0,24},{9,1},{17,9},{25,17},{1,25},{10,2},{18... | collective-permute-start | bytes 245768 | tf_op jit(solution)/shard_map/ppermute | solution.py:748
  22.3 3.0 %collective-permute-done.lo_ref = f32[5,32,128]{2,1,0:T(8,128)S(1)} collective-permute-done((f32[5,32,128]{2,1,0:T(8,128)S(1)}, f32[5,32,128]{2,1,0:T(8,128)S(1)}, u32[]{:S(2)}, u32[]{:S(2)}) %collective-permute-start) | collective-permute-done | bytes 81952 | tf_op jit(solution)/shard_map/ppermute | solution.py:747
  25.3 0.9 %collective-permute-done.1.hi_ref = f32[5,32,128]{2,1,0:T(8,128)S(1)} collective-permute-done((f32[5,32,128]{2,1,0:T(8,128)S(1)}, f32[5,32,128]{2,1,0:T(8,128)S(1)}, u32[]{:S(2)}, u32[]{:S(2)}) %collective-permute-start.1) | collective-permute-done | bytes 81952 | tf_op jit(solution)/shard_map/ppermute | solution.py:748
  26.2 5.1 %shard_map.62 = (f32[5,16,32,128]{3,2,1,0:T(8,128)S(1)}, f32[5,6,32,128]{3,2,1,0:T(8,128)S(1)}, f32[2,5,16,128]{3,2,1,0:T(8,128)S(1)}) custom-call(f32[8,48,128]{2,1,0:T(8,128)S(1)} %all-to-all-done.msg_ref, f32[5,32,128]{2,1,0:T(8,128)S(1)} %collective-permute-done.lo_ref, f32[5,32,128]{2,1,0:T(8,128)S(1)} %collective-permute-done.1.hi_ref, ...), custom_call_target="tpu_custom_call" | custom-call | flops 16777216 | bytes 16777216 | tf_op jit(solution)/shard_map/pallas_call | solution.py:689
  31.4 0.0 all-to-all-done.1
  31.4 1.7 %shard_map.63 = (f32[64,128]{1,0:T(8,128)}, f32[5,4,32,128]{3,2,1,0:T(8,128)}) custom-call(f32[64,384]{1,0:T(8,128)S(1)} %bitcast.6, s32[4,8,128]{2,1,0:T(8,128)S(1)} %get-tuple-element.23.code_ref, f32[5,6,32,128]{3,2,1,0:T(8,128)S(1)} %get-tuple-element.24.near_ref, f32[5,16,32,128]{3,2,1,0:T(8,128)S(1)} %get-tuple-element.21.after_ref.plane_ref), custom_call_target="tpu_custom_call" | custom-call | flops 1048576 | bytes 1048576 | tf_op jit(solution)/shard_map/pallas_call | solution.py:689
  33.1 3.9 %all-to-all-start.2 = ((f32[8,8,128]{2,1,0:T(8,128)}), f32[8,8,128]{2,1,0:T(8,128)S(1)}, u32[]{:S(2)}, u32[]{:S(2)}) async-start(f32[8,8,128]{2,1,0:T(8,128)} %bitcast.10), calls=%async_computation.2 | async-start | bytes 65536 | tf_op jit(solution)/shard_map/all_to_all | solution.py:814
  37.0 4.6 %shard_map.64 = f32[5,32,2048]{2,1,0:T(8,128)} custom-call(f32[5,32,2048]{2,1,0:T(8,128)S(1)} %copy-done, f32[5,16,32,128]{3,2,1,0:T(8,128)S(1)} %get-tuple-element.21.after_ref.plane_ref, f32[5,4,32,128]{3,2,1,0:T(8,128)} %get-tuple-element.25.edge_hbm, f32[2,5,16,128]{3,2,1,0:T(8,128)S(1)} %get-tuple-element.26.ends_ref, ...), custom_call_target="tpu_custom_call" | custom-call | flops 16777216 | bytes 16777216 | tf_op jit(solution)/shard_map/pallas_call | solution.py:689
  41.6 0.3 all-to-all-done.2
  41.8 0.9 %shard_map.65 = f32[5,32,128]{2,1,0:T(8,128)} custom-call(f32[64,128]{1,0:T(8,128)S(1)} %bitcast.7, bf16[64,256]{1,0:T(8,128)(2,1)S(1)} %get-tuple-element.19.after_ref.hot_ref), custom_call_target="tpu_custom_call" | custom-call | flops 262144 | bytes 262144 | tf_op jit(solution)/shard_map/pallas_call | solution.py:689
Async XLA Ops:
  0.6 7.2 %copy-start = (f32[5,32,2048]{2,1,0:T(8,128)S(1)}, f32[5,32,2048]{2,1,0:T(8,128)}, u32[]{:S(2)}) copy-start(f32[5,32,2048]{2,1,0:T(8,128)} %fine_ref.5) | copy-start | bytes 3932164
  2.7 11.4 %all-to-all-start = ((f32[8,48,128]{2,1,0:T(8,128)}), f32[8,48,128]{2,1,0:T(8,128)S(1)}, u32[]{:S(2)}, u32[]{:S(2)}) async-start(f32[8,48,128]{2,1,0:T(8,128)} %get-tuple-element.15), calls=%async_computation | async-start | bytes 393216 | tf_op jit(solution)/shard_map/all_to_all | solution.py:744
  7.9 10.5 %copy-start.2 = (f32[5,32,128]{2,1,0:T(8,128)S(1)}, f32[5,32,128]{2,1,0:T(8,128)}, u32[]{:S(2)}) copy-start(f32[5,32,128]{2,1,0:T(8,128)} %get-tuple-element.16) | copy-start | bytes 245764
  7.9 12.2 %copy-start.1 = (f32[5,32,128]{2,1,0:T(8,128)S(1)}, f32[5,32,128]{2,1,0:T(8,128)}, u32[]{:S(2)}) copy-start(f32[5,32,128]{2,1,0:T(8,128)} %get-tuple-element.17) | copy-start | bytes 245764
  15.0 16.3 %all-to-all-start.1 = ((f32[8,8,384]{2,1,0:T(8,128)}), f32[8,8,384]{2,1,0:T(8,128)S(1)}, u32[]{:S(2)}, u32[]{:S(2)}) async-start(f32[8,8,384]{2,1,0:T(8,128)} %bitcast.9), calls=%async_computation.1 | async-start | bytes 196608 | tf_op jit(solution)/shard_map/all_to_all | solution.py:778
  18.4 6.9 %collective-permute-start = (f32[5,32,128]{2,1,0:T(8,128)S(1)}, f32[5,32,128]{2,1,0:T(8,128)S(1)}, u32[]{:S(2)}, u32[]{:S(2)}) collective-permute-start(f32[5,32,128]{2,1,0:T(8,128)S(1)} %copy-done.2), channel_id=1, source_target_pairs={{0,8},{8,16},{16,24},{24,0},{1,9},{9,17},{17,25},{25,1},{2,10},{10... | collective-permute-start | bytes 245768 | tf_op jit(solution)/shard_map/ppermute | solution.py:747
  20.1 6.2 %collective-permute-start.1 = (f32[5,32,128]{2,1,0:T(8,128)S(1)}, f32[5,32,128]{2,1,0:T(8,128)S(1)}, u32[]{:S(2)}, u32[]{:S(2)}) collective-permute-start(f32[5,32,128]{2,1,0:T(8,128)S(1)} %copy-done.1), channel_id=1, source_target_pairs={{8,0},{16,8},{24,16},{0,24},{9,1},{17,9},{25,17},{1,25},{10,2},{18... | collective-permute-start | bytes 245768 | tf_op jit(solution)/shard_map/ppermute | solution.py:748
  33.1 8.7 %all-to-all-start.2 = ((f32[8,8,128]{2,1,0:T(8,128)}), f32[8,8,128]{2,1,0:T(8,128)S(1)}, u32[]{:S(2)}, u32[]{:S(2)}) async-start(f32[8,8,128]{2,1,0:T(8,128)} %bitcast.10), calls=%async_computation.2 | async-start | bytes 65536 | tf_op jit(solution)/shard_map/all_to_all | solution.py:814

commit v4 on v3

--- a/solution.py
+++ b/solution.py
@@ -26,7 +26,7 @@
 TABLE_ROWS = NF * QUANT * CF * CF
 TABLE_PAD = 384
 TERM_ROWS = 32
-Y_EARLY = 1
+Y_EARLY = 8
 NEAR = 3
 
 
@@ -83,18 +83,16 @@
 
 
 def swap_groups(tiles, lane):
-    tiles = list(tiles)
-    bit = 0
-    while (1 << bit) < len(tiles):
-        step = 1 << bit
-        upper = ((lane >> bit) & 1) == 1
-        for i in range(len(tiles)):
-            if not i & step:
-                first, second = tiles[i], tiles[i + step]
-                tiles[i] = jnp.where(upper, pltpu.roll(second, step, 1), first)
-                tiles[i + step] = jnp.where(upper, second, pltpu.roll(first, LANES - step, 1))
-        bit += 1
-    return tiles
+    count = len(tiles)
+    tiles = [pltpu.roll(t, c, 1) if c else t for c, t in enumerate(tiles)]
+    step = 1
+    while step < count:
+        odd = lane // step % 2 == 1
+        tiles = [jnp.where(odd, tiles[(i + step) % count], tiles[i]) for i in range(count)]
+        step *= 2
+    return [
+        pltpu.roll(tiles[count - z], LANES - z, 1) if z else tiles[0] for z in range(count)
+    ]
 
 
 def count_slots(owner_ref, count_ref, members, capacity, pieces):
@@ -317,7 +315,11 @@
         low_moved = low_next
 
 
-def y_columns(j, skip, blocks, lo_ref, hi_ref, load, add):
+def groups_of(start, stop):
+    return [(at, min(ROWS, stop - at)) for at in range(start, stop, ROWS)]
+
+
+def y_columns(start, count, skip, blocks, lo_ref, hi_ref, load, add):
     sub = iota((ROWS, LANES), 0)
 
     def y_back(before, here):
@@ -331,12 +333,12 @@
         return jnp.where(sub >= ROWS - 1, after, here)
 
     ends = []
-    for k in range(ROWS):
-        at = slice((2 * (j - skip) + k // 4) * ROWS, (2 * (j - skip) + k // 4 + 1) * ROWS)
+    for k in range(count):
+        c = start + k
+        at = slice((c - skip) // 4 * ROWS, ((c - skip) // 4 + 1) * ROWS)
         if k % 4 == 0:
             low = to_primitive([lo_ref[f, at, :] for f in range(NF)])
             high = to_primitive([hi_ref[f, at, :] for f in range(NF)])
-        c = ROWS * j + k
         turn_low, turn_high = (6 - 2 * (k % 4)) % ROWS, (ROWS - 2 * (k % 4)) % ROWS
         below = [pltpu.roll(t, turn_low, 0) if turn_low else t for t in low]
         above = [pltpu.roll(t, turn_high, 0) if turn_high else t for t in high]
@@ -354,13 +356,13 @@
         state = []
         for f in range(NF):
             tile = ends[0][which][f]
-            for k in range(1, ROWS):
+            for k in range(1, count):
                 tile = jnp.where(sub == k, pltpu.roll(ends[k][which][f], k, 0), tile)
             state.append(tile)
         packed.append(state)
     top = hll(packed[0], packed[1], 1)
-    for k in range(ROWS):
-        c = ROWS * j + k
+    for k in range(count):
+        c = start + k
         flux, flux_moved = ends[k][2], ends[k][3]
         for f in range(NF):
             moved = pltpu.roll(top[f], ROWS - 1 - k, 0) if k < ROWS - 1 else top[f]
@@ -369,8 +371,8 @@
 
 
 def plane_kernel(
-    members, msg_ref, lo_ref, hi_ref, fine_ref, after_ref, wz_hbm,
-    out_ref, near_ref, ends_ref, wn_ref, sem_ref,
+    members, msg_ref, lo_hbm, hi_hbm, fine_ref, after_ref, wz_hbm,
+    out_ref, near_ref, ends_ref, wn_ref, lo_ref, hi_ref, sem_ref,
 ):
     near_copies = [
         pltpu.make_async_copy(
@@ -380,7 +382,11 @@
         )
         for i, start in enumerate((0, PS - NEAR))
     ]
-    for copy in near_copies:
+    end_copies = [
+        pltpu.make_async_copy(lo_hbm, lo_ref, sem_ref.at[2]),
+        pltpu.make_async_copy(hi_hbm, hi_ref, sem_ref.at[3]),
+    ]
+    for copy in near_copies + end_copies:
         copy.start()
     me = lax.axis_index("dev")
     chunks = fine_ref.shape[2] // LANES
@@ -446,18 +452,19 @@
         at = slice(b * ROWS, (b + 1) * ROWS)
         out_ref[f, c, at, :] = out_ref[f, c, at, :] - DT_DX * change
 
-    first = 2 * ROWS * Y_EARLY
-    ends_ref[0] = lo_ref[:, first:, :]
-    ends_ref[1] = hi_ref[:, first:, :]
-    for j in range(Y_EARLY):
-        y_columns(j, 0, blocks, lo_ref, hi_ref, load, add)
+    for copy in end_copies:
+        copy.wait()
+    ends_ref[0] = lo_ref[:, 2 * Y_EARLY :, :]
+    ends_ref[1] = hi_ref[:, 2 * Y_EARLY :, :]
+    for start, count in groups_of(0, Y_EARLY):
+        y_columns(start, count, 0, blocks, lo_ref, hi_ref, load, add)
     for copy in near_copies:
         copy.wait()
 
 
 def face_kernel(
     slot_count, got_ref, code_ref, near_ref, after_ref, term_hbm, edge_hbm,
-    edge_ref, he_ref, rt_ref, lf_ref, g_ref, fs_ref, v_ref, term_ref, sem_ref,
+    edge_ref, he_ref, rt_ref, lf_ref, g_ref, v_ref, term_ref, sem_ref,
 ):
     lane = iota((ROWS, LANES), 1)
     sub = iota((ROWS, LANES), 0)
@@ -519,23 +526,13 @@
             half_slope = [
                 [0.5 * minmod(diff[i][f], diff[i + 1][f]) for f in range(NF)] for i in range(3)
             ]
-            flux = [
-                hll(
-                    [line[i + 1][f] + half_slope[i][f] for f in range(NF)],
-                    [line[i + 2][f] - half_slope[i + 1][f] for f in range(NF)],
-                    2,
-                )
-                for i in range(2)
-            ]
+            low = [[line[i + 1][f] + half_slope[i][f] for f in range(NF)] for i in range(2)]
+            up = [[line[i + 2][f] - half_slope[i + 1][f] for f in range(NF)] for i in range(2)]
+            flux = hll(low[s], up[s], 2)
+            state = low[1] if s == 0 else up[0]
             for f in range(NF):
-                if s == 0:
-                    edge_ref[f, 0, rows, :] = flux[1][f] - flux[0][f]
-                    edge_ref[f, 1, rows, :] = -flux[1][f]
-                    fs_ref[0, f, rows, :] = flux[0][f]
-                else:
-                    edge_ref[f, 2, rows, :] = flux[0][f]
-                    edge_ref[f, 3, rows, :] = flux[1][f] - flux[0][f]
-                    fs_ref[1, f, rows, :] = flux[1][f]
+                edge_ref[f, 2 * s, rows, :] = flux[f]
+                edge_ref[f, 2 * s + 1, rows, :] = state[f]
 
     edge_copy = pltpu.make_async_copy(edge_ref, edge_hbm, sem_ref.at[1])
     edge_copy.start()
@@ -544,7 +541,7 @@
         for f in range(NF):
             total = None
             for i in range(RATIO):
-                got = fs_ref[s, f, pl.ds(i, y_cells // RATIO, stride=RATIO), :]
+                got = edge_ref[f, 2 * s, pl.ds(i, y_cells // RATIO, stride=RATIO), :]
                 total = got if total is None else total + got
             total = total * (1.0 / RATIO)
             for ky in range(patch_y):
@@ -592,7 +589,7 @@
     edge_copy.start()
     for block in range(blocks):
         wz_copy(block).start()
-    first = Y_EARLY * ROWS
+    first = Y_EARLY
 
     def load(c, b):
         at = slice(b * ROWS, (b + 1) * ROWS)
@@ -602,8 +599,8 @@
         at = slice(b * ROWS, (b + 1) * ROWS)
         extra_ref[f, c - first, at, :] = plane_ref[f, c, at, :] - DT_DX * change
 
-    for j in range(Y_EARLY, chunks // ROWS):
-        y_columns(j, Y_EARLY, blocks, ends_ref.at[0], ends_ref.at[1], load, add)
+    for start, count in groups_of(first, chunks):
+        y_columns(start, count, first, blocks, ends_ref.at[0], ends_ref.at[1], load, add)
 
     edge_copy.wait()
 
@@ -614,28 +611,33 @@
         def load(z):
             return [wz_ref[f, z, rows, :] for f in range(NF)]
 
+        def edge(i):
+            return [edge_ref[f, i, rows, :] for f in range(NF)]
+
         w_here = load(1)
         w_before = load(0)
         diff = [w_here[f] - w_before[f] for f in range(NF)]
-        low = flux = None
-        for z in range(1, PS - 1):
-            w_next = load(z + 1)
-            diff_next = [w_next[f] - w_here[f] for f in range(NF)]
-            half = [0.5 * minmod(diff[f], diff_next[f]) for f in range(NF)]
-            if z >= 2:
-                new = hll(low, [w_here[f] - half[f] for f in range(NF)], 2)
-                for f in range(NF):
-                    before = edge_ref[f, 1, rows, :] if z == 2 else -flux[f]
-                    zc_ref[f, z - 2] = new[f] + before
-                flux = new
-            low = [w_here[f] + half[f] for f in range(NF)]
-            w_here, diff = w_next, diff_next
+        flux, low = edge(0), edge(1)
+        for z in range(1, PS):
+            if z < PS - 1:
+                w_next = load(z + 1)
+                diff_next = [w_next[f] - w_here[f] for f in range(NF)]
+                half = [0.5 * minmod(diff[f], diff_next[f]) for f in range(NF)]
+                up = [w_here[f] - half[f] for f in range(NF)]
+            else:
+                up = edge(3)
+            new = hll(low, up, 2)
+            for f in range(NF):
+                zc_ref[f, z - 1] = new[f] - flux[f]
+            flux = new
+            if z < PS - 1:
+                low = [w_here[f] + half[f] for f in range(NF)]
+                w_here, diff = w_next, diff_next
+        new = edge(2)
         for f in range(NF):
-            zc_ref[f, PS - 3] = edge_ref[f, 2, rows, :] - flux[f]
+            zc_ref[f, PS - 1] = new[f] - flux[f]
         for f in range(NF):
-            tiles = [edge_ref[f, 0, rows, :]]
-            tiles += [zc_ref[f, z] for z in range(PS - 2)]
-            tiles += [edge_ref[f, 3, rows, :]]
+            tiles = [zc_ref[f, z] for z in range(PS)]
             tiles = swap_groups(tiles, lane)
             for c in range(chunks):
                 at = slice(c * LANES, (c + 1) * LANES)
@@ -779,16 +781,18 @@
 
     plane, near, ends = call(
         functools.partial(plane_kernel, members),
-        (VM, VM, VM, VM, VM, HB),
+        (VM, HB, HB, VM, VM, HB),
         [
             shaped(NF, chunks, y_cells, LANES),
             shaped(NF, 2 * NEAR, y_cells, LANES),
-            shaped(2, NF, edge_rows - 2 * ROWS * Y_EARLY, LANES),
+            shaped(2, NF, edge_rows - 2 * Y_EARLY, LANES),
         ],
         (VM, VM, VM),
         [
             vmem(NF, chunks, y_cells, LANES),
-            dma((2,)),
+            vmem(*edge_shape),
+            vmem(*edge_shape),
+            dma((4,)),
         ],
         cost=1 << 24,
     )(got, y_low, y_high, fine_state, hot_box, wz)
@@ -804,7 +808,6 @@
             vmem(TABLE_PAD, slots),
             vmem(rows_all, CF * slots),
             vmem(rows_all, wide),
-            vmem(SIDES, NF, y_cells, LANES),
             vmem(TERM_ROWS, wide),
             vmem(slots, LANES),
             dma((2,)),
@@ -821,8 +824,8 @@
         [
             vmem(NF, 4, y_cells, LANES),
             vmem(*turned_shape),
-            vmem(NF, PS - 2, ROWS, LANES),
-            vmem(NF, chunks - Y_EARLY * ROWS, y_cells, LANES),
+            vmem(NF, PS, ROWS, LANES),
+            vmem(NF, chunks - Y_EARLY, y_cells, LANES),
             vmem(*fine_shape),
             dma((blocks + 1,)),
             dma((blocks,)),

time: 43.2 us -> 43.7 us (1.012)
  Pallas kernels: 19 us -> 16.7 us
  waiting for transfers between devices: 6.7 us -> 8.94 us
  local copies, waits for them, and re-layouts: 0.01 us -> 0.65 us
    pallas_call x7, Pallas kernels: 19 us -> 16.7 us  [run(): kernel(*[pltpu.with_memory_space_constraint(a, pltpu.HBM) if spec is HB e...]
    all_to_all x1, waiting for transfers between devices: 2.52 us -> 3.79 us  [local(): got = lax.all_to_all(msg, 'dev', split_axis=0, concat_axis=0, tiled=True)]
    all_to_all x1, waiting for transfers between devices: 0.26 us -> 1.23 us  [local(): lax.all_to_all(terms, 'dev', split_axis=0, concat_axis=0, tiled=True)]
    unnamed x6 -> x10, local copies, waits for them, and re-layouts: 0.01 us -> 0.65 us
  transfers between devices with their start and end apart: 5 -> 5, of which waited for: 4 -> 4; matrix products, arithmetic and copies ran while one was open for 0% -> 0% of each run, Pallas kernels for 31% -> 26%
where the time goes in v4:
time: 43.7 us; the launch traced here: 43.3 us
  Pallas kernels  16.7 us (38%)
  starting transfers between devices  16.3 us (37%)
  waiting for transfers between devices  8.94 us (20%)
  between operations  0.73 us (2%)
  local copies, waits for them, and re-layouts  0.65 us (1%)
    pallas_call x7, Pallas kernels, run(): kernel(*[pltpu.with_memory_space_constraint(a, pltpu.HBM) if spec is HB e...  16.7 us
    all_to_all x1, starting transfers between devices, local(): got = lax.all_to_all(msg, 'dev', split_axis=0, concat_axis=0, tiled=True)  5.21 us
    all_to_all x1, starting transfers between devices, local(): lax.all_to_all(terms, 'dev', split_axis=0, concat_axis=0, tiled=True)  3.86 us
    all_to_all x1, waiting for transfers between devices, local(): got = lax.all_to_all(msg, 'dev', split_axis=0, concat_axis=0, tiled=True)  3.79 us
    all_to_all x1, starting transfers between devices, local(): lax.all_to_all(payload, 'dev', split_axis=0, concat_axis=0, tiled=True)  3.37 us
    ppermute x1, waiting for transfers between devices, local(): y_low = lax.ppermute(high_edge, 'group', up)  3.01 us
    ppermute x1, starting transfers between devices, local(): y_high = lax.ppermute(low_edge, 'group', down)  2.25 us
    ppermute x1, starting transfers between devices, local(): y_low = lax.ppermute(high_edge, 'group', up)  1.63 us
  transfers between devices with their start and end apart: 5, of which 4 were waited for; matrix products, arithmetic and copies ran while one was open for 0% of the time, Pallas kernels for 26%

profile of v4, /device:TPU:0, one launch (start us, length us, event | category | flops | bytes accessed | tf_op | source)
XLA Modules:
  0.0 43.3 jit_solution(13267428841036730243)
XLA Ops:
  0.6 0.0 copy-start
  0.6 2.0 %shard_map.59 = (f32[8,48,128]{2,1,0:T(8,128)}, f32[5,32,128]{2,1,0:T(8,128)}, f32[5,32,128]{2,1,0:T(8,128)}, s32[4,8,128]{2,1,0:T(8,128)S(1)}) custom-call(s32[32]{0:T(128)} %bitcast.11, s32[32]{0:T(128)} %box_hbm.1, f32[5,32,2048]{2,1,0:T(8,128)} %fine_ref.5), custom_call_target="tpu_custom_call" | custom-call | flops 262144 | bytes 262144 | tf_op jit(solution)/shard_map/pallas_call | solution.py:691
  2.7 5.2 %all-to-all-start = ((f32[8,48,128]{2,1,0:T(8,128)}), f32[8,48,128]{2,1,0:T(8,128)S(1)}, u32[]{:S(2)}, u32[]{:S(2)}) async-start(f32[8,48,128]{2,1,0:T(8,128)} %get-tuple-element.15), calls=%async_computation | async-start | bytes 393216 | tf_op jit(solution)/shard_map/all_to_all | solution.py:746
  7.9 0.0 copy-done
  7.9 0.0 copy-start.4
  7.9 0.0 copy-start.3
  7.9 2.4 %shard_map.60 = (f32[5,16,32,128]{3,2,1,0:T(8,128)}, f32[320,256]{1,0:T(8,128)S(1)}) custom-call(f32[5,32,2048]{2,1,0:T(8,128)S(1)} %copy-done, f32[5,128,512]{2,1,0:T(8,128)} %bitcast.8), custom_call_target="tpu_custom_call" | custom-call | flops 8388608 | bytes 8388608 | tf_op jit(solution)/shard_map/pallas_call | solution.py:691
  10.3 3.8 %all-to-all-done.msg_ref = f32[8,48,128]{2,1,0:T(8,128)S(1)} async-done(((f32[8,48,128]{2,1,0:T(8,128)}), f32[8,48,128]{2,1,0:T(8,128)S(1)}, u32[]{:S(2)}, u32[]{:S(2)}) %all-to-all-start) | async-done | bytes 196640 | tf_op jit(solution)/shard_map/all_to_all | solution.py:746
  14.1 1.0 %shard_map.61 = (f32[64,384]{1,0:T(8,128)}, bf16[64,256]{1,0:T(8,128)(2,1)S(1)}) custom-call(f32[8,48,128]{2,1,0:T(8,128)S(1)} %all-to-all-done.msg_ref, f32[320,256]{1,0:T(8,128)S(1)} %get-tuple-element.18.tab_ref), custom_call_target="tpu_custom_call" | custom-call | flops 262144 | bytes 262144 | tf_op jit(solution)/shard_map/pallas_call | solution.py:691
  15.0 3.4 %all-to-all-start.1 = ((f32[8,8,384]{2,1,0:T(8,128)}), f32[8,8,384]{2,1,0:T(8,128)S(1)}, u32[]{:S(2)}, u32[]{:S(2)}) async-start(f32[8,8,384]{2,1,0:T(8,128)} %bitcast.9), calls=%async_computation.1 | async-start | bytes 196608 | tf_op jit(solution)/shard_map/all_to_all | solution.py:780
  18.4 0.0 copy-done.4
  18.4 1.6 %collective-permute-start = (f32[5,32,128]{2,1,0:T(8,128)S(1)}, f32[5,32,128]{2,1,0:T(8,128)S(1)}, u32[]{:S(2)}, u32[]{:S(2)}) collective-permute-start(f32[5,32,128]{2,1,0:T(8,128)S(1)} %copy-done.4), channel_id=1, source_target_pairs={{0,8},{8,16},{16,24},{24,0},{1,9},{9,17},{17,25},{25,1},{2,10},{10... | collective-permute-start | bytes 245768 | tf_op jit(solution)/shard_map/ppermute | solution.py:749
  20.1 0.0 copy-done.3
  20.1 2.2 %collective-permute-start.1 = (f32[5,32,128]{2,1,0:T(8,128)S(1)}, f32[5,32,128]{2,1,0:T(8,128)S(1)}, u32[]{:S(2)}, u32[]{:S(2)}) collective-permute-start(f32[5,32,128]{2,1,0:T(8,128)S(1)} %copy-done.3), channel_id=1, source_target_pairs={{8,0},{16,8},{24,16},{0,24},{9,1},{17,9},{25,17},{1,25},{10,2},{18... | collective-permute-start | bytes 245768 | tf_op jit(solution)/shard_map/ppermute | solution.py:750
  22.3 3.0 %collective-permute-done.lo_hbm = f32[5,32,128]{2,1,0:T(8,128)S(1)} collective-permute-done((f32[5,32,128]{2,1,0:T(8,128)S(1)}, f32[5,32,128]{2,1,0:T(8,128)S(1)}, u32[]{:S(2)}, u32[]{:S(2)}) %collective-permute-start) | collective-permute-done | bytes 81952 | tf_op jit(solution)/shard_map/ppermute | solution.py:749
  25.3 0.0 copy-start.1
  25.3 0.9 %collective-permute-done.1.hi_hbm = f32[5,32,128]{2,1,0:T(8,128)S(1)} collective-permute-done((f32[5,32,128]{2,1,0:T(8,128)S(1)}, f32[5,32,128]{2,1,0:T(8,128)S(1)}, u32[]{:S(2)}, u32[]{:S(2)}) %collective-permute-start.1) | collective-permute-done | bytes 81952 | tf_op jit(solution)/shard_map/ppermute | solution.py:750
  26.2 0.0 copy-start.2
  26.2 0.0 copy-done.1
  26.2 0.6 %copy-done.2 = f32[5,32,128]{2,1,0:T(8,128)} copy-done((f32[5,32,128]{2,1,0:T(8,128)}, f32[5,32,128]{2,1,0:T(8,128)S(1)}, u32[]{:S(2)}) %copy-start.2) | copy-done | bytes 81944
  26.9 5.2 %shard_map.62 = (f32[5,16,32,128]{3,2,1,0:T(8,128)S(1)}, f32[5,6,32,128]{3,2,1,0:T(8,128)S(1)}, f32[2,5,16,128]{3,2,1,0:T(8,128)S(1)}) custom-call(f32[8,48,128]{2,1,0:T(8,128)S(1)} %all-to-all-done.msg_ref, f32[5,32,128]{2,1,0:T(8,128)} %copy-done.1, f32[5,32,128]{2,1,0:T(8,128)} %copy-done.2, f32[5,32,2048]{2,1,0:T(8,128)S(1)} %copy-done, ...), custom_call_target="tpu_custom_call" | custom-call | flops 16777216 | bytes 16777216 | tf_op jit(solution)/shard_map/pallas_call | solution.py:691
  32.0 0.0 all-to-all-done.1
  32.0 1.6 %shard_map.63 = (f32[64,128]{1,0:T(8,128)}, f32[5,4,32,128]{3,2,1,0:T(8,128)}) custom-call(f32[64,384]{1,0:T(8,128)S(1)} %bitcast.6, s32[4,8,128]{2,1,0:T(8,128)S(1)} %get-tuple-element.23.code_ref, f32[5,6,32,128]{3,2,1,0:T(8,128)S(1)} %get-tuple-element.24.near_ref, f32[5,16,32,128]{3,2,1,0:T(8,128)S(1)} %get-tuple-element.21.after_ref.plane_ref), custom_call_target="tpu_custom_call" | custom-call | flops 1048576 | bytes 1048576 | tf_op jit(solution)/shard_map/pallas_call | solution.py:691
  33.7 3.9 %all-to-all-start.2 = ((f32[8,8,128]{2,1,0:T(8,128)}), f32[8,8,128]{2,1,0:T(8,128)S(1)}, u32[]{:S(2)}, u32[]{:S(2)}) async-start(f32[8,8,128]{2,1,0:T(8,128)} %bitcast.10), calls=%async_computation.2 | async-start | bytes 65536 | tf_op jit(solution)/shard_map/all_to_all | solution.py:817
  37.5 3.6 %shard_map.64 = f32[5,32,2048]{2,1,0:T(8,128)} custom-call(f32[5,32,2048]{2,1,0:T(8,128)S(1)} %copy-done, f32[5,16,32,128]{3,2,1,0:T(8,128)S(1)} %get-tuple-element.21.after_ref.plane_ref, f32[5,4,32,128]{3,2,1,0:T(8,128)} %get-tuple-element.25.edge_hbm, f32[2,5,16,128]{3,2,1,0:T(8,128)S(1)} %get-tuple-element.26.ends_ref, ...), custom_call_target="tpu_custom_call" | custom-call | flops 16777216 | bytes 16777216 | tf_op jit(solution)/shard_map/pallas_call | solution.py:691
  41.2 1.2 %all-to-all-done.2 = f32[8,8,128]{2,1,0:T(8,128)S(1)} async-done(((f32[8,8,128]{2,1,0:T(8,128)}), f32[8,8,128]{2,1,0:T(8,128)S(1)}, u32[]{:S(2)}, u32[]{:S(2)}) %all-to-all-start.2) | async-done | bytes 32800 | tf_op jit(solution)/shard_map/all_to_all | solution.py:817
  42.4 0.9 %shard_map.65 = f32[5,32,128]{2,1,0:T(8,128)} custom-call(f32[64,128]{1,0:T(8,128)S(1)} %bitcast.7, bf16[64,256]{1,0:T(8,128)(2,1)S(1)} %get-tuple-element.19.after_ref.hot_ref), custom_call_target="tpu_custom_call" | custom-call | flops 262144 | bytes 262144 | tf_op jit(solution)/shard_map/pallas_call | solution.py:691
Async XLA Ops:
  0.6 7.3 %copy-start = (f32[5,32,2048]{2,1,0:T(8,128)S(1)}, f32[5,32,2048]{2,1,0:T(8,128)}, u32[]{:S(2)}) copy-start(f32[5,32,2048]{2,1,0:T(8,128)} %fine_ref.5) | copy-start | bytes 3932164
  2.7 11.4 %all-to-all-start = ((f32[8,48,128]{2,1,0:T(8,128)}), f32[8,48,128]{2,1,0:T(8,128)S(1)}, u32[]{:S(2)}, u32[]{:S(2)}) async-start(f32[8,48,128]{2,1,0:T(8,128)} %get-tuple-element.15), calls=%async_computation | async-start | bytes 393216 | tf_op jit(solution)/shard_map/all_to_all | solution.py:746
  7.9 10.5 %copy-start.4 = (f32[5,32,128]{2,1,0:T(8,128)S(1)}, f32[5,32,128]{2,1,0:T(8,128)}, u32[]{:S(2)}) copy-start(f32[5,32,128]{2,1,0:T(8,128)} %get-tuple-element.16) | copy-start | bytes 245764
  7.9 12.2 %copy-start.3 = (f32[5,32,128]{2,1,0:T(8,128)S(1)}, f32[5,32,128]{2,1,0:T(8,128)}, u32[]{:S(2)}) copy-start(f32[5,32,128]{2,1,0:T(8,128)} %get-tuple-element.17) | copy-start | bytes 245764
  15.0 17.0 %all-to-all-start.1 = ((f32[8,8,384]{2,1,0:T(8,128)}), f32[8,8,384]{2,1,0:T(8,128)S(1)}, u32[]{:S(2)}, u32[]{:S(2)}) async-start(f32[8,8,384]{2,1,0:T(8,128)} %bitcast.9), calls=%async_computation.1 | async-start | bytes 196608 | tf_op jit(solution)/shard_map/all_to_all | solution.py:780
  18.4 6.9 %collective-permute-start = (f32[5,32,128]{2,1,0:T(8,128)S(1)}, f32[5,32,128]{2,1,0:T(8,128)S(1)}, u32[]{:S(2)}, u32[]{:S(2)}) collective-permute-start(f32[5,32,128]{2,1,0:T(8,128)S(1)} %copy-done.4), channel_id=1, source_target_pairs={{0,8},{8,16},{16,24},{24,0},{1,9},{9,17},{17,25},{25,1},{2,10},{10... | collective-permute-start | bytes 245768 | tf_op jit(solution)/shard_map/ppermute | solution.py:749
  20.1 6.2 %collective-permute-start.1 = (f32[5,32,128]{2,1,0:T(8,128)S(1)}, f32[5,32,128]{2,1,0:T(8,128)S(1)}, u32[]{:S(2)}, u32[]{:S(2)}) collective-permute-start(f32[5,32,128]{2,1,0:T(8,128)S(1)} %copy-done.3), channel_id=1, source_target_pairs={{8,0},{16,8},{24,16},{0,24},{9,1},{17,9},{25,17},{1,25},{10,2},{18... | collective-permute-start | bytes 245768 | tf_op jit(solution)/shard_map/ppermute | solution.py:750
  25.3 0.9 %copy-start.1 = (f32[5,32,128]{2,1,0:T(8,128)}, f32[5,32,128]{2,1,0:T(8,128)S(1)}, u32[]{:S(2)}) copy-start(f32[5,32,128]{2,1,0:T(8,128)S(1)} %collective-permute-done.lo_hbm) | copy-start | bytes 245764
  26.2 0.6 %copy-start.2 = (f32[5,32,128]{2,1,0:T(8,128)}, f32[5,32,128]{2,1,0:T(8,128)S(1)}, u32[]{:S(2)}) copy-start(f32[5,32,128]{2,1,0:T(8,128)S(1)} %collective-permute-done.1.hi_hbm) | copy-start | bytes 245764
  33.7 8.7 %all-to-all-start.2 = ((f32[8,8,128]{2,1,0:T(8,128)}), f32[8,8,128]{2,1,0:T(8,128)S(1)}, u32[]{:S(2)}, u32[]{:S(2)}) async-start(f32[8,8,128]{2,1,0:T(8,128)} %bitcast.10), calls=%async_computation.2 | async-start | bytes 65536 | tf_op jit(solution)/shard_map/all_to_all | solution.py:817
